TPU v7x, 32 devices: a whole 2x2x4 slice. The times are simulated.
32 devices in a mesh: ens: 2 (over y), grid: 16 (over z, x, core).
Axes of the slice: x: 2, y: 2, z: 4, core: 2. Of those that a mesh axis runs over, the one named last changes fastest.
Arguments:
- fields: bfloat16 [2, 384, 768, 256], P('ens', 'grid'), may hold values from -6 to 6
- mode_counts: int32 [384], P('grid'), may hold values from 96 to 384, as said below
- gain_attn: float32 [256], replicated, may hold values from 0.5 to 1.5
- w_query: bfloat16 [256, 256], replicated, may hold values from -1 to 1
- w_key: bfloat16 [256, 256], replicated, may hold values from -8 to 8
- w_value: bfloat16 [256, 256], replicated, may hold values from -0.375 to 0.375
- w_out: bfloat16 [256, 256], replicated, may hold values from -0.375 to 0.375
- gain_spec: float32 [256], replicated, may hold values from 0.5 to 1.5
- w_first: bfloat16 [2, 8, 32, 32], replicated, may hold values from -1 to 1
- w_second: bfloat16 [2, 8, 32, 32], replicated, may hold values from -1 to 1
Outputs:
- layer_out: bfloat16 [2, 384, 768, 256], P('ens', 'grid')
Inputs may be any that keep to these rules, and one draw needn't show every extreme that they name: `mode_counts`: longitude wavenumbers kept in each latitude row; some row keeps all 384.
All inputs are finite; a program needn't handle non-finite values.
Results may differ from a plain program's by a relative error of at most 0.012.
Values may be sent and summed in bfloat16 or wider, within the bound.
A program may use at most 256 MiB of HBM per device.

v0:
```python
import math

import jax
import jax.numpy as jnp
from jax import lax
from jax.sharding import PartitionSpec as P

HEAD = 32
NLAT = 384
KLON = 384
KLAT = 128


norm_eps = 1e-05


def layer_norm(inputs, gain_vec):
    widened = inputs.astype(jnp.float32)
    center = widened - jnp.mean(widened, axis=-1, keepdims=True)
    spread = jnp.mean(center * center, axis=-1, keepdims=True)
    return center * lax.rsqrt(spread + norm_eps) * gain_vec


def lon_table(points, mode_count):
    positions = jnp.arange(points, dtype=jnp.int32)
    frequency = jnp.arange(mode_count, dtype=jnp.int32)
    turn_count = positions[:, None] * frequency[None, :] % points
    angles = 2.0 * math.pi / points * turn_count.astype(jnp.float32)
    factor = 1.0 / math.sqrt(points)
    return jnp.concatenate([jnp.cos(angles) * factor, -jnp.sin(angles) * factor], axis=1).astype(
        jnp.bfloat16
    )


def lon_inverse(points, mode_count):
    positions = jnp.arange(points, dtype=jnp.int32)
    frequency = jnp.arange(mode_count, dtype=jnp.int32)
    turn_count = frequency[:, None] * positions[None, :] % points
    angles = 2.0 * math.pi / points * turn_count.astype(jnp.float32)
    weight = jnp.where(frequency == 0, 1.0, 2.0).astype(jnp.float32)[:, None] / math.sqrt(points)
    return jnp.stack([jnp.cos(angles) * weight, -jnp.sin(angles) * weight]).astype(jnp.bfloat16)


def lat_angles(row_count, mode_count):
    frequency = jnp.arange(mode_count, dtype=jnp.int32)
    frequency = jnp.where(frequency < mode_count // 2, frequency, frequency - mode_count)
    positions = jnp.arange(row_count, dtype=jnp.int32)
    turn_count = frequency[:, None] * positions[None, :] % row_count
    return 2.0 * math.pi / row_count * turn_count.astype(jnp.float32)


def lat_forward(row_count, mode_count):
    angles = lat_angles(row_count, mode_count)
    factor = 1.0 / math.sqrt(row_count)
    cosine = jnp.cos(angles) * factor
    sine_part = jnp.sin(angles) * factor
    return jnp.stack(
        [jnp.stack([cosine, sine_part], axis=1), jnp.stack([-sine_part, cosine], axis=1)]
    ).astype(jnp.bfloat16)


def lat_inverse(row_count, mode_count):
    angles = jnp.transpose(lat_angles(row_count, mode_count))
    factor = 1.0 / math.sqrt(row_count)
    cosine = jnp.cos(angles) * factor
    sine_part = jnp.sin(angles) * factor
    return jnp.stack([jnp.stack([cosine, -sine_part]), jnp.stack([sine_part, cosine])]).astype(
        jnp.bfloat16
    )


def complex_blocks(weight):
    real_part = weight[0]
    imag_part = weight[1]
    return jnp.stack([jnp.stack([real_part, imag_part]), jnp.stack([-imag_part, real_part])])


def mix_blocks(spec, big):
    blocks = spec.reshape(spec.shape[:4] + (big.shape[2], big.shape[3]))
    out_blocks = jnp.einsum("mpqkbi,psbio->msqkbo", blocks, big, preferred_element_type=jnp.float32)
    return out_blocks.reshape(spec.shape)


def mix_members(all_scores, all_values, head_count):
    members, lat_rows, lon_points, feat_dim = all_values.shape
    row_max = jnp.max(all_scores, axis=0, keepdims=True)
    exps = jnp.exp(all_scores - row_max)
    totals = jnp.sum(exps, axis=0)
    weights = exps.astype(jnp.bfloat16)
    split_values = all_values.reshape(members, lat_rows, lon_points, head_count, HEAD)
    mixed_out = jnp.einsum(
        "nmlhw,nlwhe->mlwhe", weights, split_values, preferred_element_type=jnp.float32
    )
    mixed_out = mixed_out / jnp.transpose(totals, (0, 1, 3, 2))[..., None]
    return mixed_out.astype(jnp.bfloat16).reshape(
        all_scores.shape[1], lat_rows, lon_points, feat_dim
    )


def shards(
    fields, mode_counts, gain_attn, w_query, w_key, w_value, w_out, gain_spec, w_first, w_second
):
    mem_dev, lat_dev, lon_points, feat_dim = fields.shape
    head_count = feat_dim // HEAD
    score_scale = 1.0 / math.sqrt(HEAD)
    normed = layer_norm(fields, gain_attn).astype(jnp.bfloat16)
    queries = jnp.dot(normed, w_query, preferred_element_type=jnp.float32).astype(jnp.bfloat16)
    queries = queries.reshape(mem_dev, lat_dev, lon_points, head_count, HEAD)
    own_keys = jnp.dot(normed, w_key, preferred_element_type=jnp.float32).astype(jnp.bfloat16)
    own_values = jnp.dot(normed, w_value, preferred_element_type=jnp.float32).astype(jnp.bfloat16)
    key_rows = lax.all_gather(own_keys, "ens", axis=0, tiled=True)
    split_keys = key_rows.reshape(key_rows.shape[:3] + (head_count, HEAD))
    scores = (
        jnp.einsum("mlwhe,nlwhe->nmlhw", queries, split_keys, preferred_element_type=jnp.float32)
        * score_scale
    )
    all_values = lax.all_gather(own_values, "ens", axis=0, tiled=True)
    mixed_out = mix_members(scores, all_values, head_count)
    attended = (
        fields.astype(jnp.float32) + jnp.dot(mixed_out, w_out, preferred_element_type=jnp.float32)
    ).astype(jnp.bfloat16)
    retained = (jnp.arange(KLON, dtype=jnp.int32)[None, :] < mode_counts[:, None]).astype(
        jnp.float32
    )
    normed_two = layer_norm(attended, gain_spec).astype(jnp.bfloat16)
    spectrum = jnp.einsum(
        "mlxd,xk->mlkd", normed_two, lon_table(lon_points, KLON), preferred_element_type=jnp.float32
    )
    spectrum = spectrum.reshape(mem_dev, lat_dev, 2, KLON, feat_dim)
    spectrum = (spectrum * retained[None, :, None, :, None]).astype(jnp.bfloat16)
    forward = lat_forward(NLAT, KLAT)
    inverse = lat_inverse(NLAT, KLAT)
    big_one = complex_blocks(w_first)
    big_two = complex_blocks(w_second)
    rows_spec = jnp.einsum(
        "pqrj,mjrkd->mpqkd",
        forward,
        lax.all_to_all(spectrum, "grid", split_axis=3, concat_axis=1, tiled=True),
        preferred_element_type=jnp.float32,
    ).astype(jnp.bfloat16)
    hidden = jnp.maximum(mix_blocks(rows_spec, big_one), 0.0).astype(jnp.bfloat16)
    second = mix_blocks(hidden, big_two).astype(jnp.bfloat16)
    back_rows = jnp.einsum(
        "rpjq,mpqkd->mjrkd", inverse, second, preferred_element_type=jnp.float32
    ).astype(jnp.bfloat16)
    returned = lax.all_to_all(back_rows, "grid", split_axis=1, concat_axis=3, tiled=True)
    returned = returned * retained.astype(jnp.bfloat16)[None, :, None, :, None]
    field_out = jnp.einsum(
        "mjrkd,rkx->mjxd",
        returned,
        lon_inverse(lon_points, KLON),
        preferred_element_type=jnp.float32,
    )
    return (attended.astype(jnp.float32) + field_out).astype(jnp.bfloat16)


def solution(mesh):
    in_specs = (P("ens", "grid", None, None), P("grid"), P(), P(), P(), P(), P(), P(), P(), P())
    out_specs = P("ens", "grid", None, None)
    return jax.shard_map(shards, mesh=mesh, in_specs=in_specs, out_specs=out_specs, check_vma=False)
```

profile of v0, /device:TPU:11, one launch (start us, length us, event | category | flops | bytes accessed | tf_op | source)
XLA Modules:
  0.0 1163.1 jit_solution(6597510635387888419)
XLA Ops:
  6.5 0.0 copy-start
  6.5 0.0 all-gather.7.cloned.1.call-start
  6.5 12.6 %copy.142 = bf16[1,24,768,256]{2,3,1,0:T(8,128)(2,1)} copy(bf16[1,24,768,256]{3,2,1,0:T(8,128)(2,1)} %param.10) | data formatting | bytes 18874368 | tf_op args[0]
  19.2 0.0 copy-start.2
  19.2 5.2 convert_reduce_fusion.1
  24.4 1.2 copy-done.2
  25.5 2.6 fusion.7
  28.2 0.0 copy-done.8
  28.2 0.0 copy-done.10
  28.2 11.0 convolution_convert_fusion.1
  39.2 0.0 all-gather.7.cloned.1.call-update
  39.2 0.0 all-gather.5.cloned.1.call-start
  39.2 0.8 copy-done.11
  40.1 13.7 %convolution_convert_fusion.2 = bf16[24,768,256]{2,1,0:T(8,128)(2,1)} fusion(bf16[256,256]{1,0:T(8,128)(2,1)S(1)} %copy-done.11, bf16[1,24,768,256]{2,3,1,0:T(8,128)(2,1)} %copy.142, f32[256]{0:T(256)S(1)} %copy-done.8, f32[24,768]{1,0:T(8,128)S(1)} %add_rsqrt_fusion.1, f32[24,768]{1,0:T(8,128)S(1)} %broadcast_multiply_fusion.1), kind=kOutput, calls=%fused_computation.36 | convolution fusion | flops 2444230656 | bytes 19153920 | tf_op jit(solution)/shard_map/dot_general | solution.py:110
  53.8 0.0 all-gather.5.cloned.1.call-update
  53.8 5.3 multiply_convert_fusion.1
  59.1 0.0 copy-done.9
  59.1 0.7 fusion.85
  59.8 0.0 copy-done.4
  59.8 15.2 %bitcast_convert_fusion.3 = f32[24,8,768,32]{2,3,1,0:T(8,128)} fusion(bf16[256,256]{1,0:T(8,128)(2,1)S(1)} %copy-done.4, bf16[1,24,768,256]{2,3,1,0:T(8,128)(2,1)} %copy.142, f32[256]{0:T(256)S(1)} %copy-done.8, f32[24,768]{1,0:T(8,128)S(1)} %add_rsqrt_fusion.1, f32[24,768]{1,0:T(8,128)S(1)} %broadcast_multiply_fusion.1), kind=kOutput, calls=%fused_computation.143 | convolution fusion | flops 2448949248 | bytes 28591104 | tf_op jit(solution)/shard_map/dot_general | solution.py:107
  75.0 189.7 %all-gather.7.cloned.1.call-done = bf16[48,768,256]{2,1,0:T(8,128)(2,1)} async-done(((bf16[24,768,256]{2,1,0:T(8,128)(2,1)}), bf16[48,768,256]{2,1,0:T(8,128)(2,1)}) %all-gather.7.cloned.1.call-update) | async-done | bytes 18874384 | tf_op jit(solution)/shard_map/all_gather | solution.py:111
  264.7 24.2 %copy.207 = bf16[48,768,256]{1,2,0:T(8,128)(2,1)} copy(bf16[48,768,256]{2,1,0:T(8,128)(2,1)} %all-gather.7.cloned.1.call-done) | data formatting | bytes 37748736
  288.9 17.8 %multiply_reduce_fusion.1 = f32[24,8,768,2]{2,1,0,3:T(8,128)S(1)} fusion(bf16[24,8,768,32,2]{2,3,1,0,4:T(8,128)(2,1)} %bitcast.170, f32[24,8,768,32]{2,3,1,0:T(8,128)} %bitcast_convert_fusion.3), kind=kLoop, calls=%fused_computation.1 | loop fusion | flops 28016640 | bytes 38928384
  306.7 0.1 bitcast_reduce_fusion
  306.8 0.2 fusion.56
  307.1 183.5 %all-gather.5.cloned.1.call-done = bf16[48,768,256]{2,1,0:T(8,128)(2,1)} async-done(((bf16[24,768,256]{2,1,0:T(8,128)(2,1)}), bf16[48,768,256]{2,1,0:T(8,128)(2,1)}) %all-gather.5.cloned.1.call-update) | async-done | bytes 18874384 | tf_op jit(solution)/shard_map/all_gather | solution.py:117
  490.6 24.6 %copy.206 = bf16[48,768,256]{1,2,0:T(8,128)(2,1)} copy(bf16[48,768,256]{2,1,0:T(8,128)(2,1)} %all-gather.5.cloned.1.call-done) | data formatting | bytes 37748736
  515.2 13.5 %multiply_reduce_fusion = f32[24,768,8,32]{1,3,2,0:T(8,128)S(1)} fusion(bf16[24,768,8,2,32]{1,4,2,0,3:T(8,128)(2,1)} %bitcast.171, f32[24,768,8,2]{1,2,3,0:T(8,128)S(1)} %get-tuple-element.6), kind=kLoop, calls=%fused_computation | loop fusion | flops 23592960 | bytes 38928384 | tf_op jit(solution)/shard_map/nmlhw,nlwhe->mlwhe/dot_general | solution.py:91
  528.8 4.8 divide_convert_fusion
  533.6 0.0 copy-done
  533.6 20.6 %convert_reduce_fusion = (f32[24,768]{1,0:T(8,128)S(1)}, bf16[1,24,768,256]{2,3,1,0:T(8,128)(2,1)}) fusion(bf16[24,768,256]{1,2,0:T(8,128)(2,1)} %bitcast.172, bf16[256,256]{1,0:T(8,128)(2,1)S(1)} %copy-done, bf16[1,24,768,256]{2,3,1,0:T(8,128)(2,1)} %copy.142), kind=kOutput, calls=%fused_computation.4 | convolution fusion | flops 2439493632 | bytes 28516352 | tf_op jit(solution)/shard_map/dot_general | solution.py:120
  554.2 0.0 copy-start.3
  554.2 0.0 copy-start.12
  554.2 6.4 fusion.4
  560.6 0.0 copy-done.3
  560.6 0.0 copy-done.12
  560.6 10.8 fusion.15
  571.4 7.6 multiply_convert_fusion
  579.0 39.1 %copy.160 = bf16[1,24,2,384,256]{4,2,1,0,3:T(2,128)(2,1)} copy(bf16[1,24,2,384,256]{4,3,2,1,0:T(8,128)(2,1)S(1)} %multiply_convert_fusion) | data formatting | bytes 18874368 | tf_op jit(solution)/shard_map/convert_element_type | solution.py:130
  618.1 6.6 all-to-all-start
  624.8 0.0 copy-done.5
  624.8 0.1 copy.156
  624.9 0.0 copy-done.6
  624.9 0.1 copy.153
  625.2 0.9 fusion.78
  626.1 0.9 negate_convert_fusion
  627.0 202.5 %all-to-all-done = bf16[1,24,2,384,256]{4,2,1,0,3:T(2,128)(2,1)} async-done(((bf16[1,24,2,384,256]{4,2,1,0,3:T(2,128)(2,1)}), bf16[1,24,2,384,256]{4,2,1,0,3:T(2,128)(2,1)}, u32[]{:S(2)}, u32[]{:S(2)}) %all-to-all-start) | async-done | bytes 9437216 | tf_op jit(solution)/shard_map/all_to_all | solution.py:138
  829.6 10.7 copy.161
  840.3 8.3 copy.162
  848.6 19.5 %bitcast_convert_fusion.2 = bf16[24,256,2,128]{3,1,2,0:T(8,128)(2,1)S(1)} fusion(bf16[384,2,24,256,1]{3,2,1,0,4:T(8,128)(2,1)} %bitcast.178, bf16[1,128,2,384]{3,1,2,0:T(8,128)(2,1)S(1)} %get-tuple-element.14, bf16[1,128,2,384]{3,1,2,0:T(8,128)(2,1)S(1)} %get-tuple-element.13), kind=kOutput, calls=%fused_computation.40 | convolution fusion | flops 2418278400 | bytes 12976128 | tf_op jit(solution)/shard_map/pqrj,mjrkd->mpqkd/dot_general | solution.py:135
  868.1 1.0 fusion.28
  869.1 1.0 fusion.29
  870.1 1.0 copy.166
  871.1 5.3 fusion.12
  876.4 24.0 %copy.168 = bf16[1,384,2,24,256]{4,2,3,0,1:T(2,128)(2,1)} copy(bf16[1,384,2,24,256]{1,4,2,3,0:T(8,128)(2,1)} %fusion.12) | data formatting | bytes 18874368 | tf_op jit(solution)/shard_map/convert_element_type | solution.py:145
  900.3 5.2 all-to-all-start.1
  905.5 5.1 multiply_convert_fusion.4
  910.6 199.5 %all-to-all-done.1 = bf16[1,384,2,24,256]{4,2,3,0,1:T(2,128)(2,1)} async-done(((bf16[1,384,2,24,256]{4,2,3,0,1:T(2,128)(2,1)}), bf16[1,384,2,24,256]{4,2,3,0,1:T(2,128)(2,1)}, u32[]{:S(2)}, u32[]{:S(2)}) %all-to-all-start.1) | async-done | bytes 9437216 | tf_op jit(solution)/shard_map/all_to_all | solution.py:146
  1110.2 8.9 copy.169
  1119.1 8.6 copy.170
  1127.7 0.0 copy-done.7
  1127.7 15.6 %fusion.11 = bf16[1,24,768,256]{2,3,1,0:T(8,128)(2,1)} fusion(bf16[1,24,768,256]{2,3,1,0:T(8,128)(2,1)} %get-tuple-element.26, bf16[24,2,384,256]{3,2,1,0:T(8,128)(2,1)} %bitcast.177, bf16[24,384]{1,0:T(8,128)(2,1)S(1)} %copy-done.7, bf16[1,384,768]{1,2,0:T(8,128)(2,1)S(1)} %get-tuple-element.16, bf16[1,384,768]{1,2,0:T(8,128)(2,1)S(1)} %get-tuple-element.15), kind=kOutput, calls=%fused_computation.19 | convolution fusion | flops 7283146752 | bytes 29509632 | tf_op jit(solution)/shard_map/mjrkd,rkx->mjxd/dot_general | solution.py:148
  1143.3 12.6 %copy.172 = bf16[1,24,768,256]{3,2,1,0:T(8,128)(2,1)} copy(bf16[1,24,768,256]{2,3,1,0:T(8,128)(2,1)} %fusion.11) | data formatting | bytes 18874368 | tf_op jit(solution)/shard_map/convert_element_type | solution.py:154
  1155.8 0.0 copy-done.1
  (21 shorter events, 0.2 us)
Async XLA Ops:
  6.5 527.0 %copy-start = (bf16[256,256]{1,0:T(8,128)(2,1)S(1)}, bf16[256,256]{1,0:T(8,128)(2,1)}, u32[]{:S(2)}) copy-start(bf16[256,256]{1,0:T(8,128)(2,1)} %param.16) | copy-start | bytes 393220
  6.5 258.1 %all-gather.7.cloned.1.call-start = ((), (), s32[]{:S(2)}) async-start(), calls=%async_computation.3 | async-start | bytes 28311552 | tf_op jit(solution)/shard_map/all_gather | solution.py:111
  19.2 6.4 copy-start.2
  19.2 9.0 copy-start.8
  19.2 9.0 copy-start.10
  39.2 0.9 copy-start.11
  39.2 451.4 %all-gather.5.cloned.1.call-start = ((), (), s32[]{:S(2)}) async-start(), calls=%async_computation.2 | async-start | bytes 28311552 | tf_op jit(solution)/shard_map/all_gather | solution.py:117
  53.8 5.3 copy-start.9
  53.8 6.0 copy-start.4
  554.2 6.5 copy-start.3
  554.2 6.5 copy-start.12
  618.1 6.6 copy-start.5
  618.1 6.8 copy-start.6
  618.1 211.5 %all-to-all-start = ((bf16[1,24,2,384,256]{4,2,1,0,3:T(2,128)(2,1)}), bf16[1,24,2,384,256]{4,2,1,0,3:T(2,128)(2,1)}, u32[]{:S(2)}, u32[]{:S(2)}) async-start(bf16[1,24,2,384,256]{4,2,1,0,3:T(2,128)(2,1)} %copy.160), calls=%async_computation | async-start | bytes 18874368 | tf_op jit(solution)/shard_map/all_to_all | solution.py:138
  900.3 209.9 %all-to-all-start.1 = ((bf16[1,384,2,24,256]{4,2,3,0,1:T(2,128)(2,1)}), bf16[1,384,2,24,256]{4,2,3,0,1:T(2,128)(2,1)}, u32[]{:S(2)}, u32[]{:S(2)}) async-start(bf16[1,384,2,24,256]{4,2,3,0,1:T(2,128)(2,1)} %copy.168), calls=%async_computation.1 | async-start | bytes 18874368 | tf_op jit(solution)/shard_map/all_to_all | solution.py:146
  1119.1 8.6 copy-start.7
  1127.7 28.1 %copy-start.1 = (bf16[256,256]{1,0:T(8,128)(2,1)S(1)}, bf16[256,256]{1,0:T(8,128)(2,1)}, u32[]{:S(2)}) copy-start(bf16[256,256]{1,0:T(8,128)(2,1)} %param.16) | copy-start | bytes 393220
Sparse Core Ops, SparseCore 0:
  39.3 225.2 all-gather.6
  266.2 224.3 all-gather.4
where the time goes:
time: 1170 us; the launch traced here: 1160 us
  waiting for transfers between devices  775 us (66%)
  local copies, waits for them, and re-layouts  177 us (15%)
  matrix products  114 us (10%)
  other arithmetic  71.3 us (6%)
  between operations  14.1 us (1%)
  starting transfers between devices  11.8 us (1%)
    all_to_all x1, waiting for transfers between devices, shards(): lax.all_to_all(spectrum, 'grid', split_axis=3, concat_axis=1, tiled=True)  203 us
    all_to_all x1, waiting for transfers between devices, shards(): lax.all_to_all(back_rows, 'grid', split_axis=1, concat_axis=3, tiled=True)  200 us
    all_gather x1, waiting for transfers between devices, shards(): key_rows = lax.all_gather(own_keys, 'ens', axis=0, tiled=True)  190 us
    all_gather x1, waiting for transfers between devices, shards(): all_values = lax.all_gather(own_values, 'ens', axis=0, tiled=True)  184 us
    unnamed x31, local copies, waits for them, and re-layouts  63.8 us
    convert_element_type x1, local copies, waits for them, and re-layouts, shards(): (spectrum * retained[None, :, None, :, None]).astype(jnp.bfloat16)  39.1 us
    convert_element_type x1, local copies, waits for them, and re-layouts, shards(): back_rows = jnp.einsum('rpjq,mpqkd->mjrkd', inverse, second, preferred_el...  24 us
  transfers between devices with their start and end apart: 4, of which 4 were waited for; matrix products, arithmetic and copies ran while one was open for 7% of the time, Pallas kernels for 0%

commit v1 on v0

v1 whole, which is shorter than its diff:
```python
import functools
import math

import jax
import jax.numpy as jnp
from jax import lax
from jax.experimental import pallas as pl
from jax.experimental.pallas import tpu as pltpu
from jax.sharding import PartitionSpec as P

HEAD = 32
NLAT = 384
KLON = 384
KLAT = 128
CHUNKS = 4

norm_eps = 1e-05


def layer_norm(widened, gain_vec):
    center = widened - jnp.mean(widened, axis=-1, keepdims=True)
    spread = jnp.mean(center * center, axis=-1, keepdims=True)
    return (center * lax.rsqrt(spread + norm_eps) * gain_vec).astype(jnp.bfloat16)


def wave_order(groups):
    held = KLON // groups
    place = jnp.arange(2 * KLON, dtype=jnp.int32)
    part = place // held % 2
    wave = place // (2 * held) * held + place % held
    return part, wave


def lon_forward(points, groups):
    part, wave = wave_order(groups)
    positions = jnp.arange(points, dtype=jnp.int32)
    turn_count = wave[:, None] * positions[None, :] % points
    angles = 2.0 * math.pi / points * turn_count.astype(jnp.float32)
    factor = 1.0 / math.sqrt(points)
    return jnp.where(
        part[:, None] == 0, jnp.cos(angles) * factor, -jnp.sin(angles) * factor
    ).astype(jnp.bfloat16)


def lon_inverse(points, groups):
    part, wave = wave_order(groups)
    positions = jnp.arange(points, dtype=jnp.int32)
    turn_count = positions[:, None] * wave[None, :] % points
    angles = 2.0 * math.pi / points * turn_count.astype(jnp.float32)
    weight = jnp.where(wave == 0, 1.0, 2.0).astype(jnp.float32)[None, :] / math.sqrt(points)
    return jnp.where(
        part[None, :] == 0, jnp.cos(angles) * weight, -jnp.sin(angles) * weight
    ).astype(jnp.bfloat16)


def lat_angles(row_count, mode_count):
    frequency = jnp.arange(mode_count, dtype=jnp.int32)
    frequency = jnp.where(frequency < mode_count // 2, frequency, frequency - mode_count)
    positions = jnp.arange(row_count, dtype=jnp.int32)
    turn_count = frequency[:, None] * positions[None, :] % row_count
    return 2.0 * math.pi / row_count * turn_count.astype(jnp.float32)


def lat_forward(row_count, mode_count):
    angles = lat_angles(row_count, mode_count)
    factor = 1.0 / math.sqrt(row_count)
    cosine = jnp.cos(angles) * factor
    sine_part = jnp.sin(angles) * factor
    return jnp.stack(
        [jnp.stack([cosine, sine_part], axis=1), jnp.stack([-sine_part, cosine], axis=1)]
    ).astype(jnp.bfloat16)


def lat_inverse(row_count, mode_count):
    angles = jnp.transpose(lat_angles(row_count, mode_count))
    factor = 1.0 / math.sqrt(row_count)
    cosine = jnp.cos(angles) * factor
    sine_part = jnp.sin(angles) * factor
    return jnp.stack([jnp.stack([cosine, -sine_part]), jnp.stack([sine_part, cosine])]).astype(
        jnp.bfloat16
    )


def complex_blocks(weight):
    real_part = weight[0]
    imag_part = weight[1]
    return jnp.stack([jnp.stack([real_part, imag_part]), jnp.stack([-imag_part, real_part])])


def mix_blocks(spec, big):
    blocks = spec.reshape(spec.shape[:3] + (big.shape[2], big.shape[3]))
    out_blocks = jnp.einsum("pqkbi,psbio->sqkbo", blocks, big, preferred_element_type=jnp.float32)
    return out_blocks.reshape(spec.shape)


def dot(left, right):
    return jnp.dot(left, right, preferred_element_type=jnp.float32)


def attend_kernel(others, first_row, sub, counts, own, *refs):
    other_refs = refs[:others]
    (gain_one, w_qkv, w_out, gain_two, table, sums, waves, attended, spectrum, normed) = refs[others:]
    points, feat = own.shape[1:]
    scale = 1.0 / math.sqrt(HEAD)
    for start in range(0, points, sub):
        rows = pl.ds(start, sub)
        fields = own[0, rows, :].astype(jnp.float32)
        joined = dot(layer_norm(fields, gain_one[...]), w_qkv[...]).astype(jnp.bfloat16)
        queries = joined[:, :feat].astype(jnp.float32)
        own_keys = joined[:, feat : 2 * feat].astype(jnp.float32)
        values = [joined[:, 2 * feat :].astype(jnp.float32)]
        shifted = [jnp.zeros((sub, feat), jnp.float32)]
        for ref in other_refs:
            side = layer_norm(ref[0, rows, :].astype(jnp.float32), gain_one[...])
            pair = dot(side, w_qkv[:, feat:]).astype(jnp.bfloat16)
            terms = queries * (pair[:, :feat].astype(jnp.float32) - own_keys)
            upper = terms.astype(jnp.bfloat16)
            lower = (terms - upper.astype(jnp.float32)).astype(jnp.bfloat16)
            total = dot(upper, sums[...]) + dot(lower, sums[...])
            shifted.append(total * scale)
            values.append(pair[:, feat:].astype(jnp.float32))
        largest = functools.reduce(jnp.maximum, shifted)
        exps = [jnp.exp(item - largest) for item in shifted]
        totals = functools.reduce(jnp.add, exps)
        mixed = functools.reduce(
            jnp.add,
            [e.astype(jnp.bfloat16).astype(jnp.float32) * v for e, v in zip(exps, values)],
        )
        mixed = (mixed / totals).astype(jnp.bfloat16)
        result = (fields + dot(mixed, w_out[...])).astype(jnp.bfloat16)
        attended[0, rows, :] = result
        normed[rows, :] = layer_norm(result.astype(jnp.float32), gain_two[...])
    kept = waves[...] < counts[first_row + pl.program_id(0)]
    spec = dot(table[...], normed[...])
    spec = jnp.where(kept, spec, 0.0).astype(jnp.bfloat16)
    if len(spectrum.shape) == 4:
        spectrum[:, 0] = spec.reshape(spectrum.shape[0], spectrum.shape[2], feat)
    else:
        spectrum[0] = spec


def attend(chunk, rows, aligned, groups, fields, others, counts, gains, weights, tables):
    points, feat = fields.shape[1:]
    first_row = chunk * rows
    sub = points // 3 if points % 48 == 0 else points
    whole = lambda a: pl.BlockSpec(a.shape, lambda i, c: (0,) * a.ndim)
    w_qkv, w_out = weights
    table, sums, waves = tables
    held = 2 * KLON // groups
    if aligned:
        spec_shape = (groups, rows, held, feat)
        spec_block = pl.BlockSpec((groups, 1, held, feat), lambda i, c: (0, i, 0, 0))
    else:
        spec_shape = (rows, 2 * KLON, feat)
        spec_block = pl.BlockSpec((1, 2 * KLON, feat), lambda i, c: (i, 0, 0))
    row_block = pl.BlockSpec((1, points, feat), lambda i, c: (i, 0, 0))
    own_block = pl.BlockSpec((1, points, feat), lambda i, c: (first_row + i, 0, 0))
    params = (gains[0], w_qkv, w_out, gains[1], table, sums, waves)
    flops = 2 * rows * points * feat * (feat * 8 + 2 * KLON)
    attended, spectrum = pl.pallas_call(
        functools.partial(attend_kernel, len(others), first_row, sub),
        grid_spec=pltpu.PrefetchScalarGridSpec(
            num_scalar_prefetch=1,
            grid=(rows,),
            in_specs=[own_block] + [row_block] * len(others) + [whole(p) for p in params],
            out_specs=[row_block, spec_block],
            scratch_shapes=[pltpu.VMEM((points, feat), jnp.bfloat16)],
        ),
        out_shape=[
            jax.ShapeDtypeStruct((rows, points, feat), jnp.bfloat16),
            jax.ShapeDtypeStruct(spec_shape, jnp.bfloat16),
        ],
        cost_estimate=pl.CostEstimate(
            flops=flops, bytes_accessed=rows * points * feat * 8, transcendentals=rows * points * feat * 2
        ),
        compiler_params=pltpu.CompilerParams(vmem_limit_bytes=40 * 1024 * 1024),
        name=f"attend_{chunk}",
    )(counts, fields, *others, *params)
    if not aligned:
        spectrum = jnp.transpose(spectrum.reshape(rows, groups, held, feat), (1, 0, 2, 3))
    return attended, spectrum


def finish_kernel(first_row, counts, spectrum, attended, table, waves, *refs):
    out = refs[-1]
    feat = out.shape[-1]
    kept = waves[...] < counts[first_row + pl.program_id(0)]
    if len(spectrum.shape) == 4:
        spec = spectrum[:, 0].reshape(2 * KLON, feat)
    else:
        spec = spectrum[0]
    spec = jnp.where(kept, spec.astype(jnp.float32), 0.0).astype(jnp.bfloat16)
    out[0] = (attended[0].astype(jnp.float32) + dot(table[...], spec)).astype(jnp.bfloat16)


def finish(chunk, rows, lat_dev, aligned, groups, spectrum, attended, counts, table, waves, so_far):
    points, feat = attended.shape[1:]
    first_row = chunk * rows
    held = 2 * KLON // groups
    whole = lambda a: pl.BlockSpec(a.shape, lambda i, c: (0,) * a.ndim)
    if aligned:
        spec_block = pl.BlockSpec((groups, 1, held, feat), lambda i, c: (0, i, 0, 0))
    else:
        spectrum = jnp.transpose(spectrum, (1, 0, 2, 3)).reshape(rows, 2 * KLON, feat)
        spec_block = pl.BlockSpec((1, 2 * KLON, feat), lambda i, c: (i, 0, 0))
    row_block = pl.BlockSpec((1, points, feat), lambda i, c: (i, 0, 0))
    out_block = pl.BlockSpec((1, points, feat), lambda i, c: (first_row + i, 0, 0))
    operands = [counts, spectrum, attended, table, waves]
    specs = [spec_block, row_block, whole(table), whole(waves)]
    aliases = {}
    if so_far is not None:
        aliases = {len(operands): 0}
        operands.append(so_far)
        specs.append(pl.BlockSpec(memory_space=pl.ANY))
    return pl.pallas_call(
        functools.partial(finish_kernel, first_row),
        grid_spec=pltpu.PrefetchScalarGridSpec(
            num_scalar_prefetch=1, grid=(rows,), in_specs=specs, out_specs=out_block
        ),
        out_shape=jax.ShapeDtypeStruct((lat_dev, points, feat), jnp.bfloat16),
        input_output_aliases=aliases,
        cost_estimate=pl.CostEstimate(
            flops=4 * rows * points * feat * KLON,
            bytes_accessed=rows * points * feat * 6,
            transcendentals=0,
        ),
        compiler_params=pltpu.CompilerParams(vmem_limit_bytes=40 * 1024 * 1024),
        name=f"finish_{chunk}",
    )(*operands)


def shards(
    mesh_sizes, fields, mode_counts, gain_attn, w_query, w_key, w_value, w_out, gain_spec, w_first, w_second
):
    members, groups = mesh_sizes
    fields = fields[0]
    lat_dev, points, feat = fields.shape
    held = KLON // groups
    aligned = (2 * held) % 16 == 0
    chunks = max(c for c in range(1, CHUNKS + 1) if lat_dev % c == 0)
    rows = lat_dev // chunks
    shifts = [
        [(i, (i + s) % members) for i in range(members)] for s in range(1, members)
    ]
    others = [
        [lax.ppermute(fields[c * rows : (c + 1) * rows], "ens", s) for s in shifts]
        for c in range(chunks)
    ]
    w_qkv = jnp.concatenate([w_query, w_key, w_value], axis=1)
    lanes = jnp.arange(feat, dtype=jnp.int32) // HEAD
    sums = (lanes[:, None] == lanes[None, :]).astype(jnp.bfloat16)
    waves = wave_order(groups)[1][:, None]
    gains = (gain_attn[None, :], gain_spec[None, :])
    tables = (lon_forward(points, groups), sums, waves)
    back_table = lon_inverse(points, groups)
    forward = lat_forward(NLAT, KLAT).reshape(2, KLAT, 2, groups, chunks, rows)
    inverse = lat_inverse(NLAT, KLAT).reshape(2, 2, groups, chunks, rows, KLAT)
    big_one = complex_blocks(w_first)
    big_two = complex_blocks(w_second)
    kept_fields = []
    rows_spec = None
    for c in range(chunks):
        attended, spectrum = attend(
            c, rows, aligned, groups, fields, others[c], mode_counts, gains, (w_qkv, w_out), tables
        )
        kept_fields.append(attended)
        arrived = lax.all_to_all(spectrum, "grid", split_axis=0, concat_axis=0)
        arrived = arrived.reshape(groups, rows, 2, held, feat)
        term = jnp.einsum(
            "pqrgj,gjrkd->pqkd",
            forward[:, :, :, :, c],
            arrived,
            preferred_element_type=jnp.float32,
        )
        rows_spec = term if rows_spec is None else rows_spec + term
    rows_spec = rows_spec.astype(jnp.bfloat16)
    hidden = jnp.maximum(mix_blocks(rows_spec, big_one), 0.0).astype(jnp.bfloat16)
    second = mix_blocks(hidden, big_two).astype(jnp.bfloat16)
    out = None
    for c in range(chunks):
        back_rows = jnp.einsum(
            "rpgjq,pqkd->gjrkd", inverse[:, :, :, c], second, preferred_element_type=jnp.float32
        ).astype(jnp.bfloat16)
        returned = lax.all_to_all(
            back_rows.reshape(groups, rows, 2 * held, feat), "grid", split_axis=0, concat_axis=0
        )
        out = finish(
            c, rows, lat_dev, aligned, groups, returned, kept_fields[c], mode_counts, back_table,
            tables[2], out,
        )
    return out[None]


def solution(mesh):
    in_specs = (P("ens", "grid", None, None), P("grid"), P(), P(), P(), P(), P(), P(), P(), P())
    out_specs = P("ens", "grid", None, None)
    sizes = (mesh.shape["ens"], mesh.shape["grid"])
    return jax.shard_map(
        functools.partial(shards, sizes),
        mesh=mesh,
        in_specs=in_specs,
        out_specs=out_specs,
        check_vma=False,
    )
```

time: 1170 us -> 657 us (0.56)
  waiting for transfers between devices: 775 us -> 388 us
  local copies, waits for them, and re-layouts: 177 us -> 40.6 us
  Pallas kernels: 0 us -> 96.5 us
  matrix products: 114 us -> 46 us
  other arithmetic: 71.3 us -> 23.2 us
  starting transfers between devices: 11.8 us -> 53.4 us
  between operations: 14.1 us -> 0.66 us
    all_gather x2 -> x0, waiting for transfers between devices: 373 us -> none  [the longest x1 190 us: shards(): key_rows = lax.all_gather(own_keys, 'ens', axis=0, tiled=True)]
    all_to_all x2 -> x8, waiting for transfers between devices: 402 us -> 203 us  [the longest x4 172 us: shards(): lax.all_to_all(back_rows.reshape(groups, rows, 2 * held, feat), 'grid', s...]
    ppermute x0 -> x4, waiting for transfers between devices: none -> 184 us  [shards(): lax.ppermute(fields[c * rows:(c + 1) * rows], 'ens', s)]
    pallas_call x0 -> x8, Pallas kernels: none -> 96.5 us  [the longest x4 68.1 us: attend(): pl.pallas_call(functools.partial(attend_kernel, len(others), first_row, s...]
    dot_general x10 -> x9, matrix products: 114 us -> 46 us  [the longest x4 30.2 us: shards(): jnp.einsum('pqrgj,gjrkd->pqkd', forward[:, :, :, :, c], arrived, preferre...]
    convert_element_type x3 -> x5, local copies, waits for them, and re-layouts: 75.6 us -> 15.9 us  [the longest x4 11.1 us: shards(): back_rows = jnp.einsum('rpgjq,pqkd->gjrkd', inverse[:, :, :, c], second,...]
    unnamed x31 -> x47, local copies, waits for them, and re-layouts: 63.8 us -> 15.3 us
    all_to_all x2 -> x8, starting transfers between devices: 11.8 us -> 48.4 us  [the longest x4 28.9 us: shards(): arrived = lax.all_to_all(spectrum, 'grid', split_axis=0, concat_axis=0)]
  transfers between devices with their start and end apart: 4 -> 12, of which waited for: 4 -> 9; matrix products, arithmetic and copies ran while one was open for 7% -> 9% of each run, Pallas kernels for 0% -> 11%
where the time goes in v1:
time: 657 us; the launch traced here: 648 us
  waiting for transfers between devices  388 us (59%)
  Pallas kernels  96.5 us (15%)
  starting transfers between devices  53.4 us (8%)
  matrix products  46 us (7%)
  local copies, waits for them, and re-layouts  40.6 us (6%)
  other arithmetic  23.2 us (4%)
    ppermute x4, waiting for transfers between devices, shards(): lax.ppermute(fields[c * rows:(c + 1) * rows], 'ens', s)  184 us
    all_to_all x4, waiting for transfers between devices, shards(): lax.all_to_all(back_rows.reshape(groups, rows, 2 * held, feat), 'grid', s...  172 us
    pallas_call x4, Pallas kernels, attend(): pl.pallas_call(functools.partial(attend_kernel, len(others), first_row, s...  68.1 us
    all_to_all x4, waiting for transfers between devices, shards(): arrived = lax.all_to_all(spectrum, 'grid', split_axis=0, concat_axis=0)  31.8 us
    dot_general x4, matrix products, shards(): jnp.einsum('pqrgj,gjrkd->pqkd', forward[:, :, :, :, c], arrived, preferre...  30.2 us
    all_to_all x4, starting transfers between devices, shards(): arrived = lax.all_to_all(spectrum, 'grid', split_axis=0, concat_axis=0)  28.9 us
    pallas_call x4, Pallas kernels, finish(): pl.pallas_call(functools.partial(finish_kernel, first_row), grid_spec=plt...  28.4 us
    convert_element_type x1, other arithmetic, lon_inverse(): return jnp.where(part[None, :] == 0, jnp.cos(angles) * weight, -jnp.sin(a...  20.6 us
  transfers between devices with their start and end apart: 12, of which 9 were waited for; matrix products, arithmetic and copies ran while one was open for 9% of the time, Pallas kernels for 11%

profile of v1, /device:TPU:11, one launch (start us, length us, event | category | flops | bytes accessed | tf_op | source)
XLA Modules:
  0.0 648.1 jit_solution(13410917291818872328)
XLA Ops:
  0.0 6.5 %slice_bitcast_fusion = (bf16[6,768,256]{2,1,0:T(8,128)(2,1)}, bf16[6,768,256]{2,1,0:T(8,128)(2,1)S(1)}, bf16[6,768,256]{2,1,0:T(8,128)(2,1)}, bf16[6,768,256]{2,1,0:T(8,128)(2,1)}) fusion(bf16[1,24,768,256]{3,2,1,0:T(8,128)(2,1)} %param.10), kind=kLoop, calls=%fused_computation.42 | loop fusion | bytes 18874368 | tf_op jit(solution)/shard_map/slice | solution.py:246
  6.5 1.2 collective-permute-start.1
  7.9 0.2 fusion.49.refs_7_.waves
  8.1 0.0 copy-start.13
  8.1 0.0 copy-start.14
  8.1 0.1 compare_convert_fusion.refs_6_
  8.2 20.6 %select_convert_fusion = (bf16[768,768]{1,0:T(8,128)(2,1)S(1)}, bf16[768,768]{1,0:T(8,128)(2,1)S(1)}) fusion(f32[768]{0:T(1024)S(1)} %select_multiply_fusion, s32[768]{0:T(1024)S(1)} %fusion.77, pred[768]{0:T(1024)(128)(4,1)S(1)} %fusion.79), kind=kLoop, calls=%fused_computation.38 | loop fusion | flops 16515072 | bytes 2366208 | tf_op jit(solution)/shard_map/convert_element_type | solution.py:53
  28.9 29.8 %collective-permute-done.1.refs_0_ = bf16[6,768,256]{2,1,0:T(8,128)(2,1)S(1)} collective-permute-done((bf16[6,768,256]{2,1,0:T(8,128)(2,1)S(1)}, bf16[6,768,256]{2,1,0:T(8,128)(2,1)S(1)}, u32[]{:S(2)}, u32[]{:S(2)}) %collective-permute-start.1) | collective-permute-done | bytes 2359328 | tf_op jit(solution)/shard_map/ppermute | solution.py:246
  58.7 17.0 %attend_1.1 = (bf16[6,768,256]{2,1,0:T(8,128)(2,1)S(1)}, bf16[16,6,48,256]{3,2,1,0:T(8,128)(2,1)S(1)}) custom-call(s32[24]{0:T(128)S(1)} %copy-done.12, bf16[24,768,256]{2,1,0:T(8,128)(2,1)} %bitcast.186, bf16[6,768,256]{2,1,0:T(8,128)(2,1)S(1)} %collective-permute-done.1.refs_0_, f32[1,256]{1,0:T(1,128)S(1)} %bitcast.173, ...), custom_call_target="tpu_custom_call" | custom-call | flops 6643777536 | bytes 9437184 | tf_op jit(solution)/shard_map/attend_1/pallas_call | solution.py:160
  75.7 1.4 copy-done.5
  77.1 1.4 copy-done.6
  78.5 7.4 %all-to-all-start.1 = ((bf16[16,6,48,256]{3,2,1,0:T(8,128)(2,1)}), bf16[16,6,48,256]{3,2,1,0:T(8,128)(2,1)}, u32[]{:S(2)}, u32[]{:S(2)}) async-start(bf16[16,6,48,256]{3,2,1,0:T(8,128)(2,1)} %copy-done.5), calls=%async_computation.1 | async-start | bytes 4718592 | tf_op jit(solution)/shard_map/all_to_all | solution.py:267
  85.9 1.2 collective-permute-start
  87.2 51.5 %collective-permute-done.refs_0_ = bf16[6,768,256]{2,1,0:T(8,128)(2,1)S(1)} collective-permute-done((bf16[6,768,256]{2,1,0:T(8,128)(2,1)}, bf16[6,768,256]{2,1,0:T(8,128)(2,1)S(1)}, u32[]{:S(2)}, u32[]{:S(2)}) %collective-permute-start) | collective-permute-done | bytes 2359328 | tf_op jit(solution)/shard_map/ppermute | solution.py:246
  138.7 17.0 %attend_0.1 = (bf16[6,768,256]{2,1,0:T(8,128)(2,1)S(1)}, bf16[16,6,48,256]{3,2,1,0:T(8,128)(2,1)S(1)}) custom-call(s32[24]{0:T(128)S(1)} %copy-done.12, bf16[24,768,256]{2,1,0:T(8,128)(2,1)} %bitcast.187, bf16[6,768,256]{2,1,0:T(8,128)(2,1)S(1)} %collective-permute-done.refs_0_, f32[1,256]{1,0:T(1,128)S(1)} %bitcast.174, ...), custom_call_target="tpu_custom_call" | custom-call | flops 6643777536 | bytes 9437184 | tf_op jit(solution)/shard_map/attend_0/pallas_call | solution.py:160
  155.7 1.4 copy-done
  157.0 1.4 copy-done.4
  158.5 7.5 %all-to-all-start = ((bf16[16,6,48,256]{3,2,1,0:T(8,128)(2,1)}), bf16[16,6,48,256]{3,2,1,0:T(8,128)(2,1)}, u32[]{:S(2)}, u32[]{:S(2)}) async-start(bf16[16,6,48,256]{3,2,1,0:T(8,128)(2,1)} %copy-done.4), calls=%async_computation | async-start | bytes 4718592 | tf_op jit(solution)/shard_map/all_to_all | solution.py:267
  165.9 1.3 collective-permute-start.2
  167.3 51.4 %collective-permute-done.2.refs_0_ = bf16[6,768,256]{2,1,0:T(8,128)(2,1)S(1)} collective-permute-done((bf16[6,768,256]{2,1,0:T(8,128)(2,1)}, bf16[6,768,256]{2,1,0:T(8,128)(2,1)S(1)}, u32[]{:S(2)}, u32[]{:S(2)}) %collective-permute-start.2) | collective-permute-done | bytes 2359328 | tf_op jit(solution)/shard_map/ppermute | solution.py:246
  218.7 17.0 %attend_2.1 = (bf16[6,768,256]{2,1,0:T(8,128)(2,1)S(1)}, bf16[16,6,48,256]{3,2,1,0:T(8,128)(2,1)S(1)}) custom-call(s32[24]{0:T(128)S(1)} %copy-done.12, bf16[24,768,256]{2,1,0:T(8,128)(2,1)} %bitcast.188, bf16[6,768,256]{2,1,0:T(8,128)(2,1)S(1)} %collective-permute-done.2.refs_0_, f32[1,256]{1,0:T(1,128)S(1)} %bitcast.175, ...), custom_call_target="tpu_custom_call" | custom-call | flops 6643777536 | bytes 9437184 | tf_op jit(solution)/shard_map/attend_2/pallas_call | solution.py:160
  235.7 1.4 copy-done.3
  237.1 1.4 copy-done.8
  238.6 6.8 %all-to-all-start.2 = ((bf16[16,6,48,256]{3,2,1,0:T(8,128)(2,1)}), bf16[16,6,48,256]{3,2,1,0:T(8,128)(2,1)}, u32[]{:S(2)}, u32[]{:S(2)}) async-start(bf16[16,6,48,256]{3,2,1,0:T(8,128)(2,1)} %copy-done.3), calls=%async_computation.2 | async-start | bytes 4718592 | tf_op jit(solution)/shard_map/all_to_all | solution.py:267
  245.4 1.2 collective-permute-start.3
  246.6 51.5 %collective-permute-done.3.refs_0_ = bf16[6,768,256]{2,1,0:T(8,128)(2,1)S(1)} collective-permute-done((bf16[6,768,256]{2,1,0:T(8,128)(2,1)}, bf16[6,768,256]{2,1,0:T(8,128)(2,1)S(1)}, u32[]{:S(2)}, u32[]{:S(2)}) %collective-permute-start.3) | collective-permute-done | bytes 2359328 | tf_op jit(solution)/shard_map/ppermute | solution.py:246
  298.1 17.0 %attend_3.1 = (bf16[6,768,256]{2,1,0:T(8,128)(2,1)S(1)}, bf16[16,6,48,256]{3,2,1,0:T(8,128)(2,1)S(1)}) custom-call(s32[24]{0:T(128)S(1)} %copy-done.12, bf16[24,768,256]{2,1,0:T(8,128)(2,1)} %bitcast.189, bf16[6,768,256]{2,1,0:T(8,128)(2,1)S(1)} %collective-permute-done.3.refs_0_, f32[1,256]{1,0:T(1,128)S(1)} %bitcast.176, ...), custom_call_target="tpu_custom_call" | custom-call | flops 6643777536 | bytes 9437184 | tf_op jit(solution)/shard_map/attend_3/pallas_call | solution.py:160
  315.2 1.4 copy-done.2
  316.6 1.5 copy-done.10
  318.1 7.2 %all-to-all-start.3 = ((bf16[16,6,48,256]{3,2,1,0:T(8,128)(2,1)}), bf16[16,6,48,256]{3,2,1,0:T(8,128)(2,1)}, u32[]{:S(2)}, u32[]{:S(2)}) async-start(bf16[16,6,48,256]{3,2,1,0:T(8,128)(2,1)} %copy-done.2), calls=%async_computation.3 | async-start | bytes 4718592 | tf_op jit(solution)/shard_map/all_to_all | solution.py:267
  325.3 0.1 copy.25
  325.6 1.0 negate_convert_fusion
  326.7 1.0 fusion.68
  327.8 6.3 fusion.22
  334.0 6.2 fusion.26
  340.3 6.3 fusion.24
  346.5 31.8 %all-to-all-done.3 = bf16[16,6,48,256]{3,2,1,0:T(8,128)(2,1)} async-done(((bf16[16,6,48,256]{3,2,1,0:T(8,128)(2,1)}), bf16[16,6,48,256]{3,2,1,0:T(8,128)(2,1)}, u32[]{:S(2)}, u32[]{:S(2)}) %all-to-all-start.3) | async-done | bytes 2359328 | tf_op jit(solution)/shard_map/all_to_all | solution.py:267
  378.3 11.4 %fusion = bf16[2,128,24,256]{3,1,2,0:T(8,128)(2,1)} fusion(f32[2,128,24,256,1,1]{3,1,5,4,2,0:T(8,128)} %fusion.22, f32[2,128,24,256,1,1]{3,1,5,4,2,0:T(8,128)} %fusion.24, f32[2,128,24,256,1,1]{3,1,5,4,2,0:T(8,128)} %fusion.26, bf16[16,6,2,24,256]{4,3,2,1,0:T(8,128)(2,1)} %bitcast.38, bf16[2,128,2,16,4,6]{1,3,2,5,0,4:T(8,128)(2,1)S(1)} %maximum_maximum_fusion), kind=kOutput, calls=%fused_computation.1 | convolution fusion | flops 610271232 | bytes 24477696 | tf_op jit(solution)/shard_map/pqrgj,gjrkd->pqkd/dot_general | solution.py:269
  389.7 4.8 copy.32
  394.5 5.4 fusion.5
  399.9 2.9 copy.33
  402.8 1.2 fusion.18
  404.0 0.5 copy-done.16
  404.4 2.8 copy.37
  407.2 4.8 all-to-all-start.5
  412.0 3.1 fusion.19
  415.1 2.7 copy.39
  417.8 47.3 %all-to-all-done.5.spectrum = bf16[16,6,48,256]{3,2,1,0:T(8,128)(2,1)} async-done(((bf16[16,6,48,256]{3,2,1,0:T(8,128)(2,1)}), bf16[16,6,48,256]{3,2,1,0:T(8,128)(2,1)}, u32[]{:S(2)}, u32[]{:S(2)}) %all-to-all-start.5) | async-done | bytes 2359328 | tf_op jit(solution)/shard_map/all_to_all | solution.py:284
  465.1 4.8 all-to-all-start.6
  469.9 3.1 fusion.20
  473.0 2.8 copy.41
  475.8 47.3 %all-to-all-done.6.spectrum = bf16[16,6,48,256]{3,2,1,0:T(8,128)(2,1)} async-done(((bf16[16,6,48,256]{3,2,1,0:T(8,128)(2,1)}), bf16[16,6,48,256]{3,2,1,0:T(8,128)(2,1)}, u32[]{:S(2)}, u32[]{:S(2)}) %all-to-all-start.6) | async-done | bytes 2359328 | tf_op jit(solution)/shard_map/all_to_all | solution.py:284
  523.0 5.2 all-to-all-start.7
  528.2 3.1 fusion.17
  531.3 2.8 copy.35
  534.1 47.1 %all-to-all-done.7.spectrum = bf16[16,6,48,256]{3,2,1,0:T(8,128)(2,1)} async-done(((bf16[16,6,48,256]{3,2,1,0:T(8,128)(2,1)}), bf16[16,6,48,256]{3,2,1,0:T(8,128)(2,1)}, u32[]{:S(2)}, u32[]{:S(2)}) %all-to-all-start.7) | async-done | bytes 2359328 | tf_op jit(solution)/shard_map/all_to_all | solution.py:284
  581.2 4.8 all-to-all-start.4
  586.0 1.7 copy-done.1
  587.6 7.2 %finish_0.1.refs_0_ = bf16[24,768,256]{2,1,0:T(8,128)(2,1)} custom-call(s32[24]{0:T(128)S(1)} %copy-done.12, bf16[16,6,48,256]{3,2,1,0:T(8,128)(2,1)} %all-to-all-done.7.spectrum, bf16[6,768,256]{2,1,0:T(8,128)(2,1)S(1)} %copy-done.1, bf16[768,768]{1,0:T(8,128)(2,1)S(1)} %get-tuple-element.35.table, s32[768,1]{1,0:T(8,128)S(1)} %fusion.49.refs_7_.waves), custom_call_target="tpu_custom_call" | custom-call | flops 1811939328 | bytes 7077888 | tf_op jit(solution)/shard_map/finish_0/pallas_call | solution.py:215
  594.8 7.2 %finish_1.1.refs_0_ = bf16[24,768,256]{2,1,0:T(8,128)(2,1)} custom-call(s32[24]{0:T(128)S(1)} %copy-done.12, bf16[16,6,48,256]{3,2,1,0:T(8,128)(2,1)} %all-to-all-done.6.spectrum, bf16[6,768,256]{2,1,0:T(8,128)(2,1)S(1)} %copy-done.7, bf16[768,768]{1,0:T(8,128)(2,1)S(1)} %get-tuple-element.35.table, ...), custom_call_target="tpu_custom_call", output_to_operand_aliasing={{}: (5, {})} | custom-call | flops 1811939328 | bytes 7077888 | tf_op jit(solution)/shard_map/finish_1/pallas_call | solution.py:215
  602.0 7.0 %finish_2.1.refs_0_ = bf16[24,768,256]{2,1,0:T(8,128)(2,1)} custom-call(s32[24]{0:T(128)S(1)} %copy-done.12, bf16[16,6,48,256]{3,2,1,0:T(8,128)(2,1)} %all-to-all-done.5.spectrum, bf16[6,768,256]{2,1,0:T(8,128)(2,1)S(1)} %copy-done.9, bf16[768,768]{1,0:T(8,128)(2,1)S(1)} %get-tuple-element.35.table, ...), custom_call_target="tpu_custom_call", output_to_operand_aliasing={{}: (5, {})} | custom-call | flops 1811939328 | bytes 7077888 | tf_op jit(solution)/shard_map/finish_2/pallas_call | solution.py:215
  609.0 30.1 %all-to-all-done.4.spectrum = bf16[16,6,48,256]{3,2,1,0:T(8,128)(2,1)} async-done(((bf16[16,6,48,256]{3,2,1,0:T(8,128)(2,1)}), bf16[16,6,48,256]{3,2,1,0:T(8,128)(2,1)}, u32[]{:S(2)}, u32[]{:S(2)}) %all-to-all-start.4) | async-done | bytes 2359328 | tf_op jit(solution)/shard_map/all_to_all | solution.py:284
  639.1 1.7 copy-done.11
  640.8 7.0 %finish_3.1 = bf16[24,768,256]{2,1,0:T(8,128)(2,1)} custom-call(s32[24]{0:T(128)S(1)} %copy-done.12, bf16[16,6,48,256]{3,2,1,0:T(8,128)(2,1)} %all-to-all-done.4.spectrum, bf16[6,768,256]{2,1,0:T(8,128)(2,1)S(1)} %copy-done.11, bf16[768,768]{1,0:T(8,128)(2,1)S(1)} %get-tuple-element.35.table, ...), custom_call_target="tpu_custom_call", output_to_operand_aliasing={{}: (5, {})} | custom-call | flops 1811939328 | bytes 7077888 | tf_op jit(solution)/shard_map/finish_3/pallas_call | solution.py:215
  (49 shorter events, 0.3 us)
Async XLA Ops:
  0.0 7.8 %copy-start.18 = (bf16[256,256]{1,0:T(8,128)(2,1)S(1)}, bf16[256,256]{1,0:T(8,128)(2,1)}, u32[]{:S(2)}) copy-start(bf16[256,256]{1,0:T(8,128)(2,1)} %param.13) | copy-start | bytes 393220
  0.0 7.8 %copy-start.19 = (bf16[256,256]{1,0:T(8,128)(2,1)S(1)}, bf16[256,256]{1,0:T(8,128)(2,1)}, u32[]{:S(2)}) copy-start(bf16[256,256]{1,0:T(8,128)(2,1)} %param.14) | copy-start | bytes 393220
  0.0 7.9 %copy-start.20 = (bf16[256,256]{1,0:T(8,128)(2,1)S(1)}, bf16[256,256]{1,0:T(8,128)(2,1)}, u32[]{:S(2)}) copy-start(bf16[256,256]{1,0:T(8,128)(2,1)} %param.15) | copy-start | bytes 393220
  6.5 52.1 %collective-permute-start.1 = (bf16[6,768,256]{2,1,0:T(8,128)(2,1)S(1)}, bf16[6,768,256]{2,1,0:T(8,128)(2,1)S(1)}, u32[]{:S(2)}, u32[]{:S(2)}) collective-permute-start(bf16[6,768,256]{2,1,0:T(8,128)(2,1)S(1)} %get-tuple-element.22), channel_id=1, source_target_pairs={{0,16},{16,0},{1,17},{17,1},{2,18},{18,2},{3,19},{19,3},{4,20},{20... | collective-permute-start | bytes 7077896 | tf_op jit(solution)/shard_map/ppermute | solution.py:246
  8.1 50.6 %copy-start.12 = (s32[24]{0:T(128)S(1)}, s32[24]{0:T(128)}, u32[]{:S(2)}) copy-start(s32[24]{0:T(128)} %counts.15) | copy-start | bytes 292
  8.1 50.6 %copy-start.13 = (bf16[256,256]{1,0:T(8,128)(2,1)S(1)}, bf16[256,256]{1,0:T(8,128)(2,1)}, u32[]{:S(2)}) copy-start(bf16[256,256]{1,0:T(8,128)(2,1)} %refs_3_.7) | copy-start | bytes 393220
  8.1 50.5 %copy-start.14 = (f32[256]{0:T(256)S(1)}, f32[256]{0:T(256)}, u32[]{:S(2)}) copy-start(f32[256]{0:T(256)} %param.12) | copy-start | bytes 3076
  8.1 50.5 %copy-start.15 = (f32[256]{0:T(256)S(1)}, f32[256]{0:T(256)}, u32[]{:S(2)}) copy-start(f32[256]{0:T(256)} %param.17) | copy-start | bytes 3076
  75.7 1.4 copy-start.5
  77.1 1.4 copy-start.6
  78.5 79.9 %all-to-all-start.1 = ((bf16[16,6,48,256]{3,2,1,0:T(8,128)(2,1)}), bf16[16,6,48,256]{3,2,1,0:T(8,128)(2,1)}, u32[]{:S(2)}, u32[]{:S(2)}) async-start(bf16[16,6,48,256]{3,2,1,0:T(8,128)(2,1)} %copy-done.5), calls=%async_computation.1 | async-start | bytes 4718592 | tf_op jit(solution)/shard_map/all_to_all | solution.py:267
  85.9 52.7 %collective-permute-start = (bf16[6,768,256]{2,1,0:T(8,128)(2,1)}, bf16[6,768,256]{2,1,0:T(8,128)(2,1)S(1)}, u32[]{:S(2)}, u32[]{:S(2)}) collective-permute-start(bf16[6,768,256]{2,1,0:T(8,128)(2,1)} %get-tuple-element.23), channel_id=1, source_target_pairs={{0,16},{16,0},{1,17},{17,1},{2,18},{18,2},{3,19},{19,3},{4,20},{20... | collective-permute-start | bytes 7077896 | tf_op jit(solution)/shard_map/ppermute | solution.py:246
  155.6 1.4 copy-start
  157.0 1.4 copy-start.4
  158.5 80.1 %all-to-all-start = ((bf16[16,6,48,256]{3,2,1,0:T(8,128)(2,1)}), bf16[16,6,48,256]{3,2,1,0:T(8,128)(2,1)}, u32[]{:S(2)}, u32[]{:S(2)}) async-start(bf16[16,6,48,256]{3,2,1,0:T(8,128)(2,1)} %copy-done.4), calls=%async_computation | async-start | bytes 4718592 | tf_op jit(solution)/shard_map/all_to_all | solution.py:267
  165.9 52.7 %collective-permute-start.2 = (bf16[6,768,256]{2,1,0:T(8,128)(2,1)}, bf16[6,768,256]{2,1,0:T(8,128)(2,1)S(1)}, u32[]{:S(2)}, u32[]{:S(2)}) collective-permute-start(bf16[6,768,256]{2,1,0:T(8,128)(2,1)} %get-tuple-element.24), channel_id=1, source_target_pairs={{0,16},{16,0},{1,17},{17,1},{2,18},{18,2},{3,19},{19,3},{4,20},{20... | collective-permute-start | bytes 7077896 | tf_op jit(solution)/shard_map/ppermute | solution.py:246
  235.7 1.4 copy-start.3
  237.1 1.4 copy-start.8
  238.6 79.5 %all-to-all-start.2 = ((bf16[16,6,48,256]{3,2,1,0:T(8,128)(2,1)}), bf16[16,6,48,256]{3,2,1,0:T(8,128)(2,1)}, u32[]{:S(2)}, u32[]{:S(2)}) async-start(bf16[16,6,48,256]{3,2,1,0:T(8,128)(2,1)} %copy-done.3), calls=%async_computation.2 | async-start | bytes 4718592 | tf_op jit(solution)/shard_map/all_to_all | solution.py:267
  245.4 52.7 %collective-permute-start.3 = (bf16[6,768,256]{2,1,0:T(8,128)(2,1)}, bf16[6,768,256]{2,1,0:T(8,128)(2,1)S(1)}, u32[]{:S(2)}, u32[]{:S(2)}) collective-permute-start(bf16[6,768,256]{2,1,0:T(8,128)(2,1)} %get-tuple-element.21), channel_id=1, source_target_pairs={{0,16},{16,0},{1,17},{17,1},{2,18},{18,2},{3,19},{19,3},{4,20},{20... | collective-permute-start | bytes 7077896 | tf_op jit(solution)/shard_map/ppermute | solution.py:246
  315.2 1.4 copy-start.2
  316.6 1.5 copy-start.10
  318.1 7.2 %copy-start.21 = (bf16[2,8,32,32]{3,2,1,0:T(8,128)(2,1)S(1)}, bf16[2,8,32,32]{3,2,1,0:T(8,128)(2,1)}, u32[]{:S(2)}) copy-start(bf16[2,8,32,32]{3,2,1,0:T(8,128)(2,1)} %param.19) | copy-start | bytes 98308
  318.1 7.5 %copy-start.17 = (bf16[2,8,32,32]{3,2,1,0:T(8,128)(2,1)S(1)}, bf16[2,8,32,32]{3,2,1,0:T(8,128)(2,1)}, u32[]{:S(2)}) copy-start(bf16[2,8,32,32]{3,2,1,0:T(8,128)(2,1)} %param.18) | copy-start | bytes 98308
  318.1 60.2 %all-to-all-start.3 = ((bf16[16,6,48,256]{3,2,1,0:T(8,128)(2,1)}), bf16[16,6,48,256]{3,2,1,0:T(8,128)(2,1)}, u32[]{:S(2)}, u32[]{:S(2)}) async-start(bf16[16,6,48,256]{3,2,1,0:T(8,128)(2,1)} %copy-done.2), calls=%async_computation.3 | async-start | bytes 4718592 | tf_op jit(solution)/shard_map/all_to_all | solution.py:267
  402.7 1.7 copy-start.16
  407.2 57.9 %all-to-all-start.5 = ((bf16[16,6,48,256]{3,2,1,0:T(8,128)(2,1)}), bf16[16,6,48,256]{3,2,1,0:T(8,128)(2,1)}, u32[]{:S(2)}, u32[]{:S(2)}) async-start(bf16[16,6,48,256]{3,2,1,0:T(8,128)(2,1)} %bitcast.193), calls=%async_computation.5 | async-start | bytes 4718592 | tf_op jit(solution)/shard_map/all_to_all | solution.py:284
  465.1 57.9 %all-to-all-start.6 = ((bf16[16,6,48,256]{3,2,1,0:T(8,128)(2,1)}), bf16[16,6,48,256]{3,2,1,0:T(8,128)(2,1)}, u32[]{:S(2)}, u32[]{:S(2)}) async-start(bf16[16,6,48,256]{3,2,1,0:T(8,128)(2,1)} %bitcast.192), calls=%async_computation.6 | async-start | bytes 4718592 | tf_op jit(solution)/shard_map/all_to_all | solution.py:284
  523.0 58.2 %all-to-all-start.7 = ((bf16[16,6,48,256]{3,2,1,0:T(8,128)(2,1)}), bf16[16,6,48,256]{3,2,1,0:T(8,128)(2,1)}, u32[]{:S(2)}, u32[]{:S(2)}) async-start(bf16[16,6,48,256]{3,2,1,0:T(8,128)(2,1)} %bitcast.191), calls=%async_computation.7 | async-start | bytes 4718592 | tf_op jit(solution)/shard_map/all_to_all | solution.py:284
  581.2 57.9 %all-to-all-start.4 = ((bf16[16,6,48,256]{3,2,1,0:T(8,128)(2,1)}), bf16[16,6,48,256]{3,2,1,0:T(8,128)(2,1)}, u32[]{:S(2)}, u32[]{:S(2)}) async-start(bf16[16,6,48,256]{3,2,1,0:T(8,128)(2,1)} %bitcast.190), calls=%async_computation.4 | async-start | bytes 4718592 | tf_op jit(solution)/shard_map/all_to_all | solution.py:284
  586.0 1.7 copy-start.1
  587.6 7.2 %copy-start.7 = (bf16[6,768,256]{2,1,0:T(8,128)(2,1)S(1)}, bf16[6,768,256]{2,1,0:T(8,128)(2,1)}, u32[]{:S(2)}) copy-start(bf16[6,768,256]{2,1,0:T(8,128)(2,1)} %copy-done.6) | copy-start | bytes 7077892
  594.8 7.2 %copy-start.9 = (bf16[6,768,256]{2,1,0:T(8,128)(2,1)S(1)}, bf16[6,768,256]{2,1,0:T(8,128)(2,1)}, u32[]{:S(2)}) copy-start(bf16[6,768,256]{2,1,0:T(8,128)(2,1)} %copy-done.8) | copy-start | bytes 7077892
  639.1 1.7 copy-start.11

commit v2 on v1

--- a/solution.py
+++ b/solution.py
@@ -12,7 +12,8 @@
 NLAT = 384
 KLON = 384
 KLAT = 128
-CHUNKS = 4
+CHUNKS = 6
+BACK_CHUNKS = 2
 
 norm_eps = 1e-05
 
@@ -174,7 +175,6 @@
             flops=flops, bytes_accessed=rows * points * feat * 8, transcendentals=rows * points * feat * 2
         ),
         compiler_params=pltpu.CompilerParams(vmem_limit_bytes=40 * 1024 * 1024),
-        name=f"attend_{chunk}",
     )(counts, fields, *others, *params)
     if not aligned:
         spectrum = jnp.transpose(spectrum.reshape(rows, groups, held, feat), (1, 0, 2, 3))
@@ -193,16 +193,15 @@
     out[0] = (attended[0].astype(jnp.float32) + dot(table[...], spec)).astype(jnp.bfloat16)
 
 
-def finish(chunk, rows, lat_dev, aligned, groups, spectrum, attended, counts, table, waves, so_far):
-    points, feat = attended.shape[1:]
-    first_row = chunk * rows
+def finish(first_row, offset, lat_dev, aligned, groups, spectrum, attended, counts, table, waves, so_far):
+    rows, points, feat = attended.shape
     held = 2 * KLON // groups
     whole = lambda a: pl.BlockSpec(a.shape, lambda i, c: (0,) * a.ndim)
     if aligned:
-        spec_block = pl.BlockSpec((groups, 1, held, feat), lambda i, c: (0, i, 0, 0))
+        spec_block = pl.BlockSpec((groups, 1, held, feat), lambda i, c: (0, offset + i, 0, 0))
     else:
-        spectrum = jnp.transpose(spectrum, (1, 0, 2, 3)).reshape(rows, 2 * KLON, feat)
-        spec_block = pl.BlockSpec((1, 2 * KLON, feat), lambda i, c: (i, 0, 0))
+        spectrum = jnp.transpose(spectrum, (1, 0, 2, 3)).reshape(-1, 2 * KLON, feat)
+        spec_block = pl.BlockSpec((1, 2 * KLON, feat), lambda i, c: (offset + i, 0, 0))
     row_block = pl.BlockSpec((1, points, feat), lambda i, c: (i, 0, 0))
     out_block = pl.BlockSpec((1, points, feat), lambda i, c: (first_row + i, 0, 0))
     operands = [counts, spectrum, attended, table, waves]
@@ -225,7 +224,6 @@
             transcendentals=0,
         ),
         compiler_params=pltpu.CompilerParams(vmem_limit_bytes=40 * 1024 * 1024),
-        name=f"finish_{chunk}",
     )(*operands)
 
 
@@ -242,10 +240,9 @@
     shifts = [
         [(i, (i + s) % members) for i in range(members)] for s in range(1, members)
     ]
-    others = [
-        [lax.ppermute(fields[c * rows : (c + 1) * rows], "ens", s) for s in shifts]
-        for c in range(chunks)
-    ]
+    others = []
+    for c in range(chunks):
+        others.append([lax.ppermute(fields[c * rows : (c + 1) * rows], "ens", s) for s in shifts])
     w_qkv = jnp.concatenate([w_query, w_key, w_value], axis=1)
     lanes = jnp.arange(feat, dtype=jnp.int32) // HEAD
     sums = (lanes[:, None] == lanes[None, :]).astype(jnp.bfloat16)
@@ -254,7 +251,9 @@
     tables = (lon_forward(points, groups), sums, waves)
     back_table = lon_inverse(points, groups)
     forward = lat_forward(NLAT, KLAT).reshape(2, KLAT, 2, groups, chunks, rows)
-    inverse = lat_inverse(NLAT, KLAT).reshape(2, 2, groups, chunks, rows, KLAT)
+    backs = max(c for c in range(1, BACK_CHUNKS + 1) if chunks % c == 0)
+    per_back = chunks // backs
+    inverse = lat_inverse(NLAT, KLAT).reshape(2, 2, groups, backs, per_back * rows, KLAT)
     big_one = complex_blocks(w_first)
     big_two = complex_blocks(w_second)
     kept_fields = []
@@ -273,22 +272,30 @@
             preferred_element_type=jnp.float32,
         )
         rows_spec = term if rows_spec is None else rows_spec + term
+        if c < chunks - 1:
+            rows_spec = lax.optimization_barrier(rows_spec)
     rows_spec = rows_spec.astype(jnp.bfloat16)
     hidden = jnp.maximum(mix_blocks(rows_spec, big_one), 0.0).astype(jnp.bfloat16)
     second = mix_blocks(hidden, big_two).astype(jnp.bfloat16)
     out = None
-    for c in range(chunks):
+    for b in range(backs):
         back_rows = jnp.einsum(
-            "rpgjq,pqkd->gjrkd", inverse[:, :, :, c], second, preferred_element_type=jnp.float32
+            "rpgjq,pqkd->gjrkd", inverse[:, :, :, b], second, preferred_element_type=jnp.float32
         ).astype(jnp.bfloat16)
         returned = lax.all_to_all(
-            back_rows.reshape(groups, rows, 2 * held, feat), "grid", split_axis=0, concat_axis=0
+            back_rows.reshape(groups, per_back * rows, 2 * held, feat), "grid", split_axis=0, concat_axis=0
         )
-        out = finish(
-            c, rows, lat_dev, aligned, groups, returned, kept_fields[c], mode_counts, back_table,
-            tables[2], out,
-        )
+        for i in range(per_back):
+            c = b * per_back + i
+            out = finish(
+                c * rows, i * rows, lat_dev, aligned, groups, returned, kept_fields[c], mode_counts,
+                back_table, tables[2], out,
+            )
     return out[None]
+
+
+def layer(mesh_sizes, *args):
+    return shards(mesh_sizes, *args)
 
 
 def solution(mesh):
@@ -296,7 +303,7 @@
     out_specs = P("ens", "grid", None, None)
     sizes = (mesh.shape["ens"], mesh.shape["grid"])
     return jax.shard_map(
-        functools.partial(shards, sizes),
+        functools.partial(layer, sizes),
         mesh=mesh,
         in_specs=in_specs,
         out_specs=out_specs,

time: 657 us -> 665 us (1.012)
  matrix products: 46 us -> 34.5 us
  local copies, waits for them, and re-layouts: 40.6 us -> 51.2 us
  waiting for transfers between devices: 388 us -> 381 us
    all_to_all x4 -> x6, waiting for transfers between devices: 31.8 us -> 16.5 us  [shards(): arrived = lax.all_to_all(spectrum, 'grid', split_axis=0, concat_axis=0)]
    all_to_all x4 -> x6, starting transfers between devices: 28.9 us -> 41.7 us  [shards(): arrived = lax.all_to_all(spectrum, 'grid', split_axis=0, concat_axis=0)]
    all_to_all x4 -> x2, waiting for transfers between devices: 172 us -> 183 us  [shards(): lax.all_to_all(back_rows.reshape(groups, per_back * rows, 2 * held, feat)...]
    unnamed x47 -> x83, local copies, waits for them, and re-layouts: 15.3 us -> 26.8 us
    all_to_all x4 -> x2, starting transfers between devices: 19.5 us -> 9.99 us  [shards(): lax.all_to_all(back_rows.reshape(groups, per_back * rows, 2 * held, feat)...]
    dot_general x4 -> x6, matrix products: 30.2 us -> 24.4 us  [shards(): jnp.einsum('pqrgj,gjrkd->pqkd', forward[:, :, :, :, c], arrived, preferre...]
    ppermute x4 -> x6, waiting for transfers between devices: 184 us -> 181 us  [shards(): lax.ppermute(fields[c * rows:(c + 1) * rows], 'ens', s)]
    pallas_call x4 -> x6, Pallas kernels: 68.1 us -> 71.3 us  [attend(): pl.pallas_call(functools.partial(attend_kernel, len(others), first_row, s...]
  transfers between devices with their start and end apart: 12 -> 14, of which waited for: 9 -> 9; matrix products, arithmetic and copies ran while one was open for 9% -> 8% of each run, Pallas kernels for 11% -> 11%
where the time goes in v2:
time: 665 us; the launch traced here: 656 us
  waiting for transfers between devices  381 us (57%)
  Pallas kernels  103 us (15%)
  starting transfers between devices  59.3 us (9%)
  local copies, waits for them, and re-layouts  51.2 us (8%)
  matrix products  34.5 us (5%)
  other arithmetic  26.9 us (4%)
    all_to_all x2, waiting for transfers between devices, shards(): lax.all_to_all(back_rows.reshape(groups, per_back * rows, 2 * held, feat)...  183 us
    ppermute x6, waiting for transfers between devices, shards(): lax.ppermute(fields[c * rows:(c + 1) * rows], 'ens', s)  181 us
    pallas_call x6, Pallas kernels, attend(): pl.pallas_call(functools.partial(attend_kernel, len(others), first_row, s...  71.3 us
    all_to_all x6, starting transfers between devices, shards(): arrived = lax.all_to_all(spectrum, 'grid', split_axis=0, concat_axis=0)  41.7 us
    pallas_call x6, Pallas kernels, finish(): pl.pallas_call(functools.partial(finish_kernel, first_row), grid_spec=plt...  31.5 us
    unnamed x83, local copies, waits for them, and re-layouts  26.8 us
    dot_general x6, matrix products, shards(): jnp.einsum('pqrgj,gjrkd->pqkd', forward[:, :, :, :, c], arrived, preferre...  24.4 us
    convert_element_type x1, other arithmetic, lon_inverse(): return jnp.where(part[None, :] == 0, jnp.cos(angles) * weight, -jnp.sin(a...  20.6 us
  transfers between devices with their start and end apart: 14, of which 9 were waited for; matrix products, arithmetic and copies ran while one was open for 8% of the time, Pallas kernels for 11%

profile of v2, /device:TPU:11, one launch (start us, length us, event | category | flops | bytes accessed | tf_op | source)
XLA Modules:
  0.0 656.2 jit_solution(2894408332080655363)
XLA Ops:
  0.0 6.8 %slice_bitcast_fusion = (bf16[4,768,256]{2,1,0:T(8,128)(2,1)}, bf16[4,768,256]{2,1,0:T(8,128)(2,1)}, bf16[4,768,256]{2,1,0:T(8,128)(2,1)}, bf16[4,768,256]{2,1,0...) fusion(bf16[1,24,768,256]{3,2,1,0:T(8,128)(2,1)} %param.10), kind=kLoop, calls=%fused_computation.50 | loop fusion | bytes 18874368 | tf_op jit(solution)/shard_map/slice | solution.py:245
  6.8 1.2 collective-permute-start
  8.5 20.6 %select_convert_fusion = (bf16[768,768]{1,0:T(8,128)(2,1)S(1)}, bf16[768,768]{1,0:T(8,128)(2,1)S(1)}) fusion(f32[768]{0:T(1024)S(1)} %select_multiply_fusion, s32[768]{0:T(1024)S(1)} %fusion.74, pred[768]{0:T(1024)(128)(4,1)S(1)} %fusion.76), kind=kLoop, calls=%fused_computation.28 | loop fusion | flops 16515072 | bytes 2366208 | tf_op jit(solution)/shard_map/convert_element_type | solution.py:54
  29.1 12.9 %collective-permute-done.refs_0_ = bf16[4,768,256]{2,1,0:T(8,128)(2,1)S(1)} collective-permute-done((bf16[4,768,256]{2,1,0:T(8,128)(2,1)S(1)}, bf16[4,768,256]{2,1,0:T(8,128)(2,1)S(1)}, u32[]{:S(2)}, u32[]{:S(2)}) %collective-permute-start) | collective-permute-done | bytes 1572896 | tf_op jit(solution)/shard_map/ppermute | solution.py:245
  42.1 11.9 %shard_map.100 = (bf16[4,768,256]{2,1,0:T(8,128)(2,1)S(1)}, bf16[16,4,48,256]{3,2,1,0:T(8,128)(2,1)S(1)}) custom-call(s32[24]{0:T(128)S(1)} %copy-done.22, bf16[24,768,256]{2,1,0:T(8,128)(2,1)} %bitcast.192, bf16[4,768,256]{2,1,0:T(8,128)(2,1)S(1)} %collective-permute-done.refs_0_, f32[1,256]{1,0:T(1,128)S(1)} %bitcast.175, ...), custom_call_target="tpu_custom_call" | custom-call | flops 4429185024 | bytes 6291456 | tf_op jit(solution)/shard_map/pallas_call | solution.py:161
  54.0 1.1 copy-done.15
  55.2 7.4 %all-to-all-start = ((bf16[16,4,48,256]{3,2,1,0:T(8,128)(2,1)}), bf16[16,4,48,256]{3,2,1,0:T(8,128)(2,1)}, u32[]{:S(2)}, u32[]{:S(2)}) async-start(bf16[16,4,48,256]{3,2,1,0:T(8,128)(2,1)} %copy-done.15), calls=%async_computation | async-start | bytes 3145728 | tf_op jit(solution)/shard_map/all_to_all | solution.py:266
  62.5 1.2 collective-permute-start.1
  63.8 34.6 %collective-permute-done.1.refs_0_ = bf16[4,768,256]{2,1,0:T(8,128)(2,1)S(1)} collective-permute-done((bf16[4,768,256]{2,1,0:T(8,128)(2,1)}, bf16[4,768,256]{2,1,0:T(8,128)(2,1)S(1)}, u32[]{:S(2)}, u32[]{:S(2)}) %collective-permute-start.1) | collective-permute-done | bytes 1572896 | tf_op jit(solution)/shard_map/ppermute | solution.py:245
  99.4 1.3 copy-done.27
  100.7 11.9 %shard_map.101 = (bf16[4,768,256]{2,1,0:T(8,128)(2,1)S(1)}, bf16[16,4,48,256]{3,2,1,0:T(8,128)(2,1)S(1)}) custom-call(s32[24]{0:T(128)S(1)} %copy-done.22, bf16[24,768,256]{2,1,0:T(8,128)(2,1)} %bitcast.193, bf16[4,768,256]{2,1,0:T(8,128)(2,1)S(1)} %collective-permute-done.1.refs_0_, f32[1,256]{1,0:T(1,128)S(1)} %bitcast.176, ...), custom_call_target="tpu_custom_call" | custom-call | flops 4429185024 | bytes 6291456 | tf_op jit(solution)/shard_map/pallas_call | solution.py:161
  113.7 1.2 copy-done.12
  114.9 7.1 %all-to-all-start.1 = ((bf16[16,4,48,256]{3,2,1,0:T(8,128)(2,1)}), bf16[16,4,48,256]{3,2,1,0:T(8,128)(2,1)}, u32[]{:S(2)}, u32[]{:S(2)}) async-start(bf16[16,4,48,256]{3,2,1,0:T(8,128)(2,1)} %copy-done.12), calls=%async_computation.1 | async-start | bytes 3145728 | tf_op jit(solution)/shard_map/all_to_all | solution.py:266
  122.0 1.3 collective-permute-start.2
  123.3 34.5 %collective-permute-done.2.refs_0_ = bf16[4,768,256]{2,1,0:T(8,128)(2,1)S(1)} collective-permute-done((bf16[4,768,256]{2,1,0:T(8,128)(2,1)}, bf16[4,768,256]{2,1,0:T(8,128)(2,1)S(1)}, u32[]{:S(2)}, u32[]{:S(2)}) %collective-permute-start.2) | collective-permute-done | bytes 1572896 | tf_op jit(solution)/shard_map/ppermute | solution.py:245
  158.8 1.3 copy-done.28
  160.1 11.9 %shard_map.102 = (bf16[4,768,256]{2,1,0:T(8,128)(2,1)S(1)}, bf16[16,4,48,256]{3,2,1,0:T(8,128)(2,1)S(1)}) custom-call(s32[24]{0:T(128)S(1)} %copy-done.22, bf16[24,768,256]{2,1,0:T(8,128)(2,1)} %bitcast.194, bf16[4,768,256]{2,1,0:T(8,128)(2,1)S(1)} %collective-permute-done.2.refs_0_, f32[1,256]{1,0:T(1,128)S(1)} %bitcast.177, ...), custom_call_target="tpu_custom_call" | custom-call | flops 4429185024 | bytes 6291456 | tf_op jit(solution)/shard_map/pallas_call | solution.py:161
  173.1 1.2 copy-done.13
  174.3 6.9 %all-to-all-start.2 = ((bf16[16,4,48,256]{3,2,1,0:T(8,128)(2,1)}), bf16[16,4,48,256]{3,2,1,0:T(8,128)(2,1)}, u32[]{:S(2)}, u32[]{:S(2)}) async-start(bf16[16,4,48,256]{3,2,1,0:T(8,128)(2,1)} %copy-done.13), calls=%async_computation.2 | async-start | bytes 3145728 | tf_op jit(solution)/shard_map/all_to_all | solution.py:266
  181.1 1.2 collective-permute-start.3
  182.4 34.6 %collective-permute-done.3.refs_0_ = bf16[4,768,256]{2,1,0:T(8,128)(2,1)S(1)} collective-permute-done((bf16[4,768,256]{2,1,0:T(8,128)(2,1)}, bf16[4,768,256]{2,1,0:T(8,128)(2,1)S(1)}, u32[]{:S(2)}, u32[]{:S(2)}) %collective-permute-start.3) | collective-permute-done | bytes 1572896 | tf_op jit(solution)/shard_map/ppermute | solution.py:245
  218.0 1.3 copy-done.29
  219.3 11.9 %shard_map.103 = (bf16[4,768,256]{2,1,0:T(8,128)(2,1)S(1)}, bf16[16,4,48,256]{3,2,1,0:T(8,128)(2,1)S(1)}) custom-call(s32[24]{0:T(128)S(1)} %copy-done.22, bf16[24,768,256]{2,1,0:T(8,128)(2,1)} %bitcast.195, bf16[4,768,256]{2,1,0:T(8,128)(2,1)S(1)} %collective-permute-done.3.refs_0_, f32[1,256]{1,0:T(1,128)S(1)} %bitcast.178, ...), custom_call_target="tpu_custom_call" | custom-call | flops 4429185024 | bytes 6291456 | tf_op jit(solution)/shard_map/pallas_call | solution.py:161
  232.3 1.2 copy-done.14
  233.5 6.8 %all-to-all-start.3 = ((bf16[16,4,48,256]{3,2,1,0:T(8,128)(2,1)}), bf16[16,4,48,256]{3,2,1,0:T(8,128)(2,1)}, u32[]{:S(2)}, u32[]{:S(2)}) async-start(bf16[16,4,48,256]{3,2,1,0:T(8,128)(2,1)} %copy-done.14), calls=%async_computation.3 | async-start | bytes 3145728 | tf_op jit(solution)/shard_map/all_to_all | solution.py:266
  240.3 1.2 collective-permute-start.4
  241.5 34.6 %collective-permute-done.4.refs_0_ = bf16[4,768,256]{2,1,0:T(8,128)(2,1)S(1)} collective-permute-done((bf16[4,768,256]{2,1,0:T(8,128)(2,1)}, bf16[4,768,256]{2,1,0:T(8,128)(2,1)S(1)}, u32[]{:S(2)}, u32[]{:S(2)}) %collective-permute-start.4) | collective-permute-done | bytes 1572896 | tf_op jit(solution)/shard_map/ppermute | solution.py:245
  277.1 1.3 copy-done.30
  278.4 11.9 %shard_map.104 = (bf16[4,768,256]{2,1,0:T(8,128)(2,1)S(1)}, bf16[16,4,48,256]{3,2,1,0:T(8,128)(2,1)S(1)}) custom-call(s32[24]{0:T(128)S(1)} %copy-done.22, bf16[24,768,256]{2,1,0:T(8,128)(2,1)} %bitcast.196, bf16[4,768,256]{2,1,0:T(8,128)(2,1)S(1)} %collective-permute-done.4.refs_0_, f32[1,256]{1,0:T(1,128)S(1)} %bitcast.179, ...), custom_call_target="tpu_custom_call" | custom-call | flops 4429185024 | bytes 6291456 | tf_op jit(solution)/shard_map/pallas_call | solution.py:161
  290.3 1.1 copy-done.6
  291.4 1.2 copy-done.10
  292.6 6.8 %all-to-all-start.4 = ((bf16[16,4,48,256]{3,2,1,0:T(8,128)(2,1)}), bf16[16,4,48,256]{3,2,1,0:T(8,128)(2,1)}, u32[]{:S(2)}, u32[]{:S(2)}) async-start(bf16[16,4,48,256]{3,2,1,0:T(8,128)(2,1)} %copy-done.10), calls=%async_computation.4 | async-start | bytes 3145728 | tf_op jit(solution)/shard_map/all_to_all | solution.py:266
  299.4 1.2 collective-permute-start.5
  305.8 29.5 %collective-permute-done.5.refs_0_ = bf16[4,768,256]{2,1,0:T(8,128)(2,1)} collective-permute-done((bf16[4,768,256]{2,1,0:T(8,128)(2,1)}, bf16[4,768,256]{2,1,0:T(8,128)(2,1)}, u32[]{:S(2)}, u32[]{:S(2)}) %collective-permute-start.5) | collective-permute-done | bytes 1572896 | tf_op jit(solution)/shard_map/ppermute | solution.py:245
  336.2 1.3 copy-done.31
  337.5 12.0 %shard_map.105 = (bf16[4,768,256]{2,1,0:T(8,128)(2,1)S(1)}, bf16[16,4,48,256]{3,2,1,0:T(8,128)(2,1)S(1)}) custom-call(s32[24]{0:T(128)S(1)} %copy-done.22, bf16[24,768,256]{2,1,0:T(8,128)(2,1)} %bitcast.197, bf16[4,768,256]{2,1,0:T(8,128)(2,1)} %collective-permute-done.5.refs_0_, f32[1,256]{1,0:T(1,128)S(1)} %bitcast.180, bf16[256,768]{1,0:T(8,128)(2,1)S(1)} %copy-done.21, ...), custom_call_target="tpu_custom_call" | custom-call | flops 4429185024 | bytes 6291456 | tf_op jit(solution)/shard_map/pallas_call | solution.py:161
  349.5 1.1 copy-done.8
  350.7 1.2 copy-done.11
  351.8 6.9 %all-to-all-start.5 = ((bf16[16,4,48,256]{3,2,1,0:T(8,128)(2,1)}), bf16[16,4,48,256]{3,2,1,0:T(8,128)(2,1)}, u32[]{:S(2)}, u32[]{:S(2)}) async-start(bf16[16,4,48,256]{3,2,1,0:T(8,128)(2,1)} %copy-done.11), calls=%async_computation.5 | async-start | bytes 3145728 | tf_op jit(solution)/shard_map/all_to_all | solution.py:266
  360.5 3.0 convolution_bitcast_fusion
  363.5 3.1 bitcast_add_fusion.4
  366.6 3.1 bitcast_add_fusion.3
  369.6 3.1 bitcast_add_fusion.2
  372.7 5.8 bitcast_add_fusion.1
  378.5 16.5 %all-to-all-done.5 = bf16[16,4,48,256]{3,2,1,0:T(8,128)(2,1)} async-done(((bf16[16,4,48,256]{3,2,1,0:T(8,128)(2,1)}), bf16[16,4,48,256]{3,2,1,0:T(8,128)(2,1)}, u32[]{:S(2)}, u32[]{:S(2)}) %all-to-all-start.5) | async-done | bytes 1572896 | tf_op jit(solution)/shard_map/all_to_all | solution.py:266
  395.0 6.5 fusion
  401.4 4.9 copy.36
  406.4 5.4 fusion.7
  411.8 2.8 copy.37
  414.6 1.6 copy-done.32
  416.3 1.4 fusion.3
  417.7 4.9 copy.41
  422.6 4.8 all-to-all-start.7
  427.4 3.3 fusion.2
  430.7 5.0 copy.39
  435.7 95.4 %all-to-all-done.7.spectrum = bf16[16,12,48,256]{3,2,1,0:T(8,128)(2,1)} async-done(((bf16[16,12,48,256]{3,2,1,0:T(8,128)(2,1)}), bf16[16,12,48,256]{3,2,1,0:T(8,128)(2,1)}, u32[]{:S(2)}, u32[]{:S(2)}) %all-to-all-start.7) | async-done | bytes 4718624 | tf_op jit(solution)/shard_map/all_to_all | solution.py:285
  531.1 5.2 all-to-all-start.6
  536.3 5.3 shard_map.106.refs_0_
  541.6 5.3 shard_map.107.refs_0_
  546.9 5.3 shard_map.108.refs_0_
  552.1 87.8 %all-to-all-done.6.spectrum = bf16[16,12,48,256]{3,2,1,0:T(8,128)(2,1)} async-done(((bf16[16,12,48,256]{3,2,1,0:T(8,128)(2,1)}), bf16[16,12,48,256]{3,2,1,0:T(8,128)(2,1)}, u32[]{:S(2)}, u32[]{:S(2)}) %all-to-all-start.6) | async-done | bytes 4718624 | tf_op jit(solution)/shard_map/all_to_all | solution.py:285
  639.9 5.3 shard_map.109.refs_0_
  645.1 5.3 shard_map.110.refs_0_
  650.4 5.3 shard_map.111
  (92 shorter events, 15.8 us)
Async XLA Ops:
  0.0 8.1 %copy-start.37 = (bf16[256,256]{1,0:T(8,128)(2,1)S(1)}, bf16[256,256]{1,0:T(8,128)(2,1)}, u32[]{:S(2)}) copy-start(bf16[256,256]{1,0:T(8,128)(2,1)} %param.13) | copy-start | bytes 393220
  0.0 8.1 %copy-start.38 = (bf16[256,256]{1,0:T(8,128)(2,1)S(1)}, bf16[256,256]{1,0:T(8,128)(2,1)}, u32[]{:S(2)}) copy-start(bf16[256,256]{1,0:T(8,128)(2,1)} %param.14) | copy-start | bytes 393220
  0.0 8.1 %copy-start.39 = (bf16[256,256]{1,0:T(8,128)(2,1)S(1)}, bf16[256,256]{1,0:T(8,128)(2,1)}, u32[]{:S(2)}) copy-start(bf16[256,256]{1,0:T(8,128)(2,1)} %param.15) | copy-start | bytes 393220
  6.8 35.3 %collective-permute-start = (bf16[4,768,256]{2,1,0:T(8,128)(2,1)S(1)}, bf16[4,768,256]{2,1,0:T(8,128)(2,1)S(1)}, u32[]{:S(2)}, u32[]{:S(2)}) collective-permute-start(bf16[4,768,256]{2,1,0:T(8,128)(2,1)S(1)} %get-tuple-element.33), channel_id=1, source_target_pairs={{0,16},{16,0},{1,17},{17,1},{2,18},{18,2},{3,19},{19,3},{4,20},{20... | collective-permute-start | bytes 4718600 | tf_op jit(solution)/shard_map/ppermute | solution.py:245
  8.2 33.9 %copy-start.16 = (bf16[256,768]{1,0:T(8,128)(2,1)}, bf16[256,768]{1,0:T(8,128)(2,1)S(1)}, u32[]{:S(2)}) copy-start(bf16[256,768]{1,0:T(8,128)(2,1)S(1)} %constant_dynamic-update-slice_fusion.refs_2_) | copy-start | bytes 1179652
  8.4 33.7 %copy-start.22 = (s32[24]{0:T(128)S(1)}, s32[24]{0:T(128)}, u32[]{:S(2)}) copy-start(s32[24]{0:T(128)} %counts.23) | copy-start | bytes 292
  8.4 33.7 %copy-start.23 = (bf16[256,256]{1,0:T(8,128)(2,1)S(1)}, bf16[256,256]{1,0:T(8,128)(2,1)}, u32[]{:S(2)}) copy-start(bf16[256,256]{1,0:T(8,128)(2,1)} %refs_3_.11) | copy-start | bytes 393220
  8.4 33.7 %copy-start.24 = (f32[256]{0:T(256)S(1)}, f32[256]{0:T(256)}, u32[]{:S(2)}) copy-start(f32[256]{0:T(256)} %param.12) | copy-start | bytes 3076
  8.4 33.7 %copy-start.25 = (f32[256]{0:T(256)S(1)}, f32[256]{0:T(256)}, u32[]{:S(2)}) copy-start(f32[256]{0:T(256)} %param.17) | copy-start | bytes 3076
  29.1 24.9 %copy-start.26 = (bf16[768,768]{1,0:T(8,128)(2,1)}, bf16[768,768]{1,0:T(8,128)(2,1)S(1)}, u32[]{:S(2)}) copy-start(bf16[768,768]{1,0:T(8,128)(2,1)S(1)} %get-tuple-element.46.refs_5_) | copy-start | bytes 3538948
  54.0 1.2 copy-start.15
  55.2 59.7 %all-to-all-start = ((bf16[16,4,48,256]{3,2,1,0:T(8,128)(2,1)}), bf16[16,4,48,256]{3,2,1,0:T(8,128)(2,1)}, u32[]{:S(2)}, u32[]{:S(2)}) async-start(bf16[16,4,48,256]{3,2,1,0:T(8,128)(2,1)} %copy-done.15), calls=%async_computation | async-start | bytes 3145728 | tf_op jit(solution)/shard_map/all_to_all | solution.py:266
  62.5 35.9 %collective-permute-start.1 = (bf16[4,768,256]{2,1,0:T(8,128)(2,1)}, bf16[4,768,256]{2,1,0:T(8,128)(2,1)S(1)}, u32[]{:S(2)}, u32[]{:S(2)}) collective-permute-start(bf16[4,768,256]{2,1,0:T(8,128)(2,1)} %get-tuple-element.32), channel_id=1, source_target_pairs={{0,16},{16,0},{1,17},{17,1},{2,18},{18,2},{3,19},{19,3},{4,20},{20... | collective-permute-start | bytes 4718600 | tf_op jit(solution)/shard_map/ppermute | solution.py:245
  98.4 1.0 copy-start.17
  99.4 1.3 copy-start.27
  112.6 1.1 copy-start
  113.7 1.2 copy-start.12
  114.9 59.4 %all-to-all-start.1 = ((bf16[16,4,48,256]{3,2,1,0:T(8,128)(2,1)}), bf16[16,4,48,256]{3,2,1,0:T(8,128)(2,1)}, u32[]{:S(2)}, u32[]{:S(2)}) async-start(bf16[16,4,48,256]{3,2,1,0:T(8,128)(2,1)} %copy-done.12), calls=%async_computation.1 | async-start | bytes 3145728 | tf_op jit(solution)/shard_map/all_to_all | solution.py:266
  122.0 35.9 %collective-permute-start.2 = (bf16[4,768,256]{2,1,0:T(8,128)(2,1)}, bf16[4,768,256]{2,1,0:T(8,128)(2,1)S(1)}, u32[]{:S(2)}, u32[]{:S(2)}) collective-permute-start(bf16[4,768,256]{2,1,0:T(8,128)(2,1)} %get-tuple-element.31), channel_id=1, source_target_pairs={{0,16},{16,0},{1,17},{17,1},{2,18},{18,2},{3,19},{19,3},{4,20},{20... | collective-permute-start | bytes 4718600 | tf_op jit(solution)/shard_map/ppermute | solution.py:245
  157.8 1.0 copy-start.18
  158.8 1.3 copy-start.28
  171.9 1.2 copy-start.2
  173.1 1.2 copy-start.13
  174.3 59.2 %all-to-all-start.2 = ((bf16[16,4,48,256]{3,2,1,0:T(8,128)(2,1)}), bf16[16,4,48,256]{3,2,1,0:T(8,128)(2,1)}, u32[]{:S(2)}, u32[]{:S(2)}) async-start(bf16[16,4,48,256]{3,2,1,0:T(8,128)(2,1)} %copy-done.13), calls=%async_computation.2 | async-start | bytes 3145728 | tf_op jit(solution)/shard_map/all_to_all | solution.py:266
  181.1 35.9 %collective-permute-start.3 = (bf16[4,768,256]{2,1,0:T(8,128)(2,1)}, bf16[4,768,256]{2,1,0:T(8,128)(2,1)S(1)}, u32[]{:S(2)}, u32[]{:S(2)}) collective-permute-start(bf16[4,768,256]{2,1,0:T(8,128)(2,1)} %get-tuple-element.30), channel_id=1, source_target_pairs={{0,16},{16,0},{1,17},{17,1},{2,18},{18,2},{3,19},{19,3},{4,20},{20... | collective-permute-start | bytes 4718600 | tf_op jit(solution)/shard_map/ppermute | solution.py:245
  217.0 1.0 copy-start.19
  218.0 1.3 copy-start.29
  231.1 1.1 copy-start.4
  232.3 1.2 copy-start.14
  233.5 59.1 %all-to-all-start.3 = ((bf16[16,4,48,256]{3,2,1,0:T(8,128)(2,1)}), bf16[16,4,48,256]{3,2,1,0:T(8,128)(2,1)}, u32[]{:S(2)}, u32[]{:S(2)}) async-start(bf16[16,4,48,256]{3,2,1,0:T(8,128)(2,1)} %copy-done.14), calls=%async_computation.3 | async-start | bytes 3145728 | tf_op jit(solution)/shard_map/all_to_all | solution.py:266
  240.3 35.9 %collective-permute-start.4 = (bf16[4,768,256]{2,1,0:T(8,128)(2,1)}, bf16[4,768,256]{2,1,0:T(8,128)(2,1)S(1)}, u32[]{:S(2)}, u32[]{:S(2)}) collective-permute-start(bf16[4,768,256]{2,1,0:T(8,128)(2,1)} %get-tuple-element.34), channel_id=1, source_target_pairs={{0,16},{16,0},{1,17},{17,1},{2,18},{18,2},{3,19},{19,3},{4,20},{20... | collective-permute-start | bytes 4718600 | tf_op jit(solution)/shard_map/ppermute | solution.py:245
  276.1 1.0 copy-start.20
  277.1 1.3 copy-start.30
  290.3 1.2 copy-start.6
  291.4 1.2 copy-start.10
  292.6 59.2 %all-to-all-start.4 = ((bf16[16,4,48,256]{3,2,1,0:T(8,128)(2,1)}), bf16[16,4,48,256]{3,2,1,0:T(8,128)(2,1)}, u32[]{:S(2)}, u32[]{:S(2)}) async-start(bf16[16,4,48,256]{3,2,1,0:T(8,128)(2,1)} %copy-done.10), calls=%async_computation.4 | async-start | bytes 3145728 | tf_op jit(solution)/shard_map/all_to_all | solution.py:266
  299.4 35.9 %collective-permute-start.5 = (bf16[4,768,256]{2,1,0:T(8,128)(2,1)}, bf16[4,768,256]{2,1,0:T(8,128)(2,1)}, u32[]{:S(2)}, u32[]{:S(2)}) collective-permute-start(bf16[4,768,256]{2,1,0:T(8,128)(2,1)} %get-tuple-element.29), channel_id=1, source_target_pairs={{0,16},{16,0},{1,17},{17,1},{2,18},{18,2},{3,19},{19,3},{4,20},{20... | collective-permute-start | bytes 4718600 | tf_op jit(solution)/shard_map/ppermute | solution.py:245
  335.2 1.0 copy-start.21
  336.2 1.3 copy-start.31
  349.5 1.2 copy-start.8
  350.7 1.2 copy-start.11
  351.8 43.2 %all-to-all-start.5 = ((bf16[16,4,48,256]{3,2,1,0:T(8,128)(2,1)}), bf16[16,4,48,256]{3,2,1,0:T(8,128)(2,1)}, u32[]{:S(2)}, u32[]{:S(2)}) async-start(bf16[16,4,48,256]{3,2,1,0:T(8,128)(2,1)} %copy-done.11), calls=%async_computation.5 | async-start | bytes 3145728 | tf_op jit(solution)/shard_map/all_to_all | solution.py:266
  360.5 3.0 copy-start.33
  401.4 4.9 copy-start.35
  401.4 4.9 copy-start.36
  411.8 4.5 copy-start.34
  414.6 1.6 copy-start.32
  422.6 108.5 %all-to-all-start.7 = ((bf16[16,12,48,256]{3,2,1,0:T(8,128)(2,1)}), bf16[16,12,48,256]{3,2,1,0:T(8,128)(2,1)}, u32[]{:S(2)}, u32[]{:S(2)}) async-start(bf16[16,12,48,256]{3,2,1,0:T(8,128)(2,1)} %bitcast.190), calls=%async_computation.7 | async-start | bytes 9437184 | tf_op jit(solution)/shard_map/all_to_all | solution.py:285
  531.1 108.8 %all-to-all-start.6 = ((bf16[16,12,48,256]{3,2,1,0:T(8,128)(2,1)}), bf16[16,12,48,256]{3,2,1,0:T(8,128)(2,1)}, u32[]{:S(2)}, u32[]{:S(2)}) async-start(bf16[16,12,48,256]{3,2,1,0:T(8,128)(2,1)} %bitcast.189), calls=%async_computation.6 | async-start | bytes 9437184 | tf_op jit(solution)/shard_map/all_to_all | solution.py:285
  536.3 5.3 copy-start.1
  541.6 5.3 copy-start.3
  546.8 93.0 %copy-start.5 = (bf16[4,768,256]{2,1,0:T(8,128)(2,1)S(1)}, bf16[4,768,256]{2,1,0:T(8,128)(2,1)}, u32[]{:S(2)}) copy-start(bf16[4,768,256]{2,1,0:T(8,128)(2,1)} %copy-done.4) | copy-start | bytes 4718596
  639.9 5.3 copy-start.7
  645.1 5.3 copy-start.9
